TPU v7x, 512 devices: a whole 4x4x16 slice. The times are simulated.
512 devices in a mesh: group: 8 (over y, x_lo), member: 64 (over z, x_hi, core).
Axes of the slice: x: 4 (x_hi: 2, x_lo: 2; x = x_hi * 2 + x_lo), y: 4, z: 16, core: 2. Of those that a mesh axis runs over, the one named last changes fastest.
Arguments:
- student: bfloat16 [196608, 768], P(('group', 'member')), may hold values from -0.29882812 to 0.29882812
- teacher: bfloat16 [196608, 1024], P(('group', 'member')), may hold values from -14 to 14
- counts: int32 [196608], P(('group', 'member')), may hold values from 1 to 7, as said below
- plan: int32 [8, 64, 5], P('group', 'member'), may hold values from 0 to 1, as said below
Outputs:
- grad_student: float32 [196608, 768], P(('group', 'member'))
- loss: float32 [], replicated
Inputs may be any that keep to these rules, and one draw needn't show every extreme that they name: `counts`: each row's count is a whole number from 1 up. The pairing is symmetric: plan[g, m, 2 + k - 1] equals plan[g, (m + k) mod 64, k - 1] for k = 1 to 2, and plan[g, m, 4] equals plan[g xor 1, m, 4].
All inputs are finite; a program needn't handle non-finite values.
Results may differ from a plain program's by a relative error of at most 0.0046.
Values may be sent and summed in bfloat16 or wider, within the bound.
A program may use at most 64 MiB of HBM per device.

v0:
```python
import jax
import jax.numpy as jnp
from jax import lax
from jax.sharding import PartitionSpec as P

EPS = 1e-06


def passed_along(value, axis, steps):
    count = lax.axis_size(axis)
    pairs = [(source, (source + steps) % count) for source in range(count)]
    return lax.ppermute(value, axis, pairs)


def partner_2(block, axis, bit):
    count = lax.axis_size(axis)
    route = []
    for low in range(count):
        high = low | 1 << bit
        if high != low and high < count:
            route += [(low, high), (high, low)]
    return lax.ppermute(block, axis, route)


def normalize(embeddings):
    widened = embeddings.astype(jnp.float32)
    row_scale = lax.rsqrt(jnp.sum(widened * widened, axis=-1, keepdims=True) + EPS)
    return ((widened * row_scale).astype(jnp.bfloat16), row_scale)


def block_terms(local_rows, partner, switch):
    local_s, local_t, local_w = local_rows
    partner_s, partner_t, partner_w = partner
    local_count = local_s.shape[0]
    features = local_s.shape[1]

    def compute(operand):
        student_sim = jnp.einsum(
            "id,jd->ij", local_s, partner_s, preferred_element_type=jnp.float32
        )
        teacher_sim = jnp.einsum(
            "id,jd->ij", local_t, partner_t, preferred_element_type=jnp.float32
        )
        mismatch = student_sim - teacher_sim
        pair_weight = local_w[:, None] * partner_w.astype(jnp.float32)[None, :]
        coefficient = (pair_weight * mismatch).astype(jnp.bfloat16)
        contrib = jnp.dot(coefficient, partner_s, preferred_element_type=jnp.float32)
        results = (contrib, jnp.sum(pair_weight * mismatch * mismatch), jnp.sum(pair_weight))
        return results

    def skipped(operand):
        results = (
            jnp.zeros((local_count, features), jnp.float32),
            jnp.float32(0.0),
            jnp.float32(0.0),
        )
        return results

    return lax.cond(switch > 0, compute, skipped, 0)


def per_device(student, teacher, counts, plan):
    unit_student, row_scale = normalize(student)
    unit_teacher, unused_scale = normalize(teacher)
    weights = counts.astype(jnp.float32)
    switches = plan.reshape(-1).astype(jnp.float32)
    span_blocks = (switches.shape[0] - 1) // 2
    local_rows = (unit_student, unit_teacher, weights)
    outgoing = (unit_student, unit_teacher, weights.astype(jnp.bfloat16))
    summed_grad, loss_sum, weight_sum = block_terms(local_rows, outgoing, jnp.float32(1.0))
    for offset in range(1, span_blocks + 1):
        lower = passed_along((outgoing[0], outgoing[1], outgoing[2]), "member", offset)
        upper = passed_along((outgoing[0], outgoing[1], outgoing[2]), "member", -offset)
        for column, partner in ((offset - 1, lower), (span_blocks + offset - 1, upper)):
            contrib, loss_part, weight_part = block_terms(local_rows, partner, switches[column])
            summed_grad = summed_grad + contrib
            loss_sum = loss_sum + loss_part
            weight_sum = weight_sum + weight_part
    partner = partner_2((outgoing[0], outgoing[1], outgoing[2]), "group", 0)
    contrib, loss_part, weight_part = block_terms(local_rows, partner, switches[2 * span_blocks])
    summed_grad = summed_grad + contrib
    loss_sum = loss_sum + loss_part
    weight_sum = weight_sum + weight_part
    loss_sum, weight_sum = lax.psum((loss_sum, weight_sum), ("group", "member"))
    unit_float = unit_student.astype(jnp.float32)
    along_unit = jnp.sum(summed_grad * unit_float, axis=-1, keepdims=True)
    grad_student = 4.0 * row_scale * (summed_grad - along_unit * unit_float)
    loss = student.shape[1] * loss_sum / weight_sum
    return (grad_student, loss)


def solution(mesh):
    return jax.shard_map(
        per_device,
        mesh=mesh,
        in_specs=(
            P(("group", "member"), None),
            P(("group", "member"), None),
            P(("group", "member")),
            P("group", "member", None),
        ),
        out_specs=(P(("group", "member"), None), P()),
        check_vma=False,
    )
```

profile of v0, /device:TPU:1, one launch (start us, length us, event | category | flops | bytes accessed | tf_op | source)
XLA Modules:
  0.0 264.0 jit_solution(1487551678774136010)
XLA Ops:
  2.4 6.0 %collective-permute-start.2 = (bf16[384,1024]{1,0:T(8,128)(2,1)S(1)}, bf16[384,1024]{1,0:T(8,128)(2,1)S(1)}, u32[]{:S(2)}, u32[]{:S(2)}) collective-permute-start(bf16[384,1024]{1,0:T(8,128)(2,1)S(1)} %fusion.36), channel_id=1, source_target_pairs={{0,1},{1,2},{2,3},{3,4},{4,5},{5,6},{6,7},{7,8},{8,9},{9,10},{10,1... | collective-permute-start | bytes 2359304 | tf_op jit(solution)/shard_map/ppermute | solution.py:12
  8.4 4.7 %collective-permute-start.5 = (bf16[384,1024]{1,0:T(8,128)(2,1)S(1)}, bf16[384,1024]{1,0:T(8,128)(2,1)S(1)}, u32[]{:S(2)}, u32[]{:S(2)}) collective-permute-start(bf16[384,1024]{1,0:T(8,128)(2,1)S(1)} %fusion.36), channel_id=1, source_target_pairs={{0,63},{1,0},{2,1},{3,2},{4,3},{5,4},{6,5},{7,6},{8,7},{9,8},{10,9... | collective-permute-start | bytes 2359304 | tf_op jit(solution)/shard_map/ppermute | solution.py:12
  13.1 2.4 collective-permute-start
  15.5 7.4 %collective-permute-start.3 = (bf16[384]{0:T(512)(128)(2,1)S(1)}, bf16[384]{0:T(512)(128)(2,1)S(1)}, u32[]{:S(2)}, u32[]{:S(2)}) collective-permute-start(bf16[384]{0:T(512)(128)(2,1)S(1)} %get-tuple-element.139), channel_id=1, source_target_pairs={{0,63},{1,0},{2,1},{3,2},{4,3},{5,4},{6,5},{7,6},{8,7},{9,8},{10,9... | collective-permute-start | bytes 2312 | tf_op jit(solution)/shard_map/ppermute | solution.py:12
  23.0 1.9 collective-permute-start.6
  25.8 5.9 %collective-permute-start.1 = (bf16[384,768]{1,0:T(8,128)(2,1)S(1)}, bf16[384,768]{1,0:T(8,128)(2,1)S(1)}, u32[]{:S(2)}, u32[]{:S(2)}) collective-permute-start(bf16[384,768]{1,0:T(8,128)(2,1)S(1)} %fusion.38), channel_id=1, source_target_pairs={{0,1},{1,2},{2,3},{3,4},{4,5},{5,6},{6,7},{7,8},{8,9},{9,10},{10,1... | collective-permute-start | bytes 1769480 | tf_op jit(solution)/shard_map/ppermute | solution.py:12
  31.7 7.7 %collective-permute-start.9 = (bf16[384]{0:T(512)(128)(2,1)S(1)}, bf16[384]{0:T(512)(128)(2,1)S(1)}, u32[]{:S(2)}, u32[]{:S(2)}) collective-permute-start(bf16[384]{0:T(512)(128)(2,1)S(1)} %get-tuple-element.139), channel_id=1, source_target_pairs={{0,62},{1,63},{2,0},{3,1},{4,2},{5,3},{6,4},{7,5},{8,6},{9,7},{10,... | collective-permute-start | bytes 2312 | tf_op jit(solution)/shard_map/ppermute | solution.py:12
  39.5 5.4 %collective-permute-start.4 = (bf16[384,768]{1,0:T(8,128)(2,1)S(1)}, bf16[384,768]{1,0:T(8,128)(2,1)S(1)}, u32[]{:S(2)}, u32[]{:S(2)}) collective-permute-start(bf16[384,768]{1,0:T(8,128)(2,1)S(1)} %fusion.38), channel_id=1, source_target_pairs={{0,63},{1,0},{2,1},{3,2},{4,3},{5,4},{6,5},{7,6},{8,7},{9,8},{10,9... | collective-permute-start | bytes 1769480 | tf_op jit(solution)/shard_map/ppermute | solution.py:12
  44.9 1.9 collective-permute-start.7
  46.9 1.9 collective-permute-start.8
  48.8 3.4 %collective-permute-done.4 = bf16[384,768]{1,0:T(8,128)(2,1)S(1)} collective-permute-done((bf16[384,768]{1,0:T(8,128)(2,1)S(1)}, bf16[384,768]{1,0:T(8,128)(2,1)S(1)}, u32[]{:S(2)}, u32[]{:S(2)}) %collective-permute-start.4) | collective-permute-done | bytes 589856 | tf_op jit(solution)/shard_map/ppermute | solution.py:12
  52.2 10.2 %collective-permute-start.11 = (bf16[384,1024]{1,0:T(8,128)(2,1)S(1)}, bf16[384,1024]{1,0:T(8,128)(2,1)}, u32[]{:S(2)}, u32[]{:S(2)}) collective-permute-start(bf16[384,1024]{1,0:T(8,128)(2,1)S(1)} %fusion.36), channel_id=1, source_target_pairs={{0,62},{1,63},{2,0},{3,1},{4,2},{5,3},{6,4},{7,5},{8,6},{9,7},{10,... | collective-permute-start | bytes 2359304 | tf_op jit(solution)/shard_map/ppermute | solution.py:12
  62.4 2.7 %collective-permute-done.7 = bf16[384,768]{1,0:T(8,128)(2,1)S(1)} collective-permute-done((bf16[384,768]{1,0:T(8,128)(2,1)S(1)}, bf16[384,768]{1,0:T(8,128)(2,1)S(1)}, u32[]{:S(2)}, u32[]{:S(2)}) %collective-permute-start.7) | collective-permute-done | bytes 589856 | tf_op jit(solution)/shard_map/ppermute | solution.py:12
  65.9 2.2 collective-permute-start.14
  68.1 27.2 %collective-permute-start.10 = (bf16[384,768]{1,0:T(8,128)(2,1)S(1)}, bf16[384,768]{1,0:T(8,128)(2,1)}, u32[]{:S(2)}, u32[]{:S(2)}) collective-permute-start(bf16[384,768]{1,0:T(8,128)(2,1)S(1)} %fusion.38), channel_id=1, source_target_pairs={{0,62},{1,63},{2,0},{3,1},{4,2},{5,3},{6,4},{7,5},{8,6},{9,7},{10,... | collective-permute-start | bytes 1769480 | tf_op jit(solution)/shard_map/ppermute | solution.py:12
  95.3 1.9 collective-permute-start.13
  101.7 2.0 multiply_reduce_fusion.5
  103.7 5.4 %conditional.5 = (f32[384,768]{1,0:T(8,128)S(1)}, f32[]{:T(128)}, f32[]{:T(128)}) conditional(s32[]{:T(128)} %bitcast, () %tuple.48, (f32[384]{0:T(512)S(1)}, bf16[384]{0:T(512)(128)(2,1)S(1)}, bf16[384,768]{1,0:T(8,128)(2,1)S(1)}, bf16[384,768]{1,0:T(8,128)(2,1)}, bf16[384,1024]{1,0:T(8,128)(2,1)S(1)}, ...), branch_computations={%region_2.0_spmd, %region_3.6_spmd} | conditional | flops 756302208 | bytes 12394840 | solution.py:59
  104.6 1.7 fusion.51
  109.8 1.9 collective-permute-start.12
  111.7 5.9 %conditional.6 = (f32[384,768]{1,0:T(8,128)}, f32[]{:T(128)}, f32[]{:T(128)}) conditional(s32[]{:T(128)} %bitcast.1, () %tuple.50, (f32[384]{0:T(512)S(1)}, bf16[384]{0:T(512)(128)(2,1)S(1)}, bf16[384,768]{1,0:T(8,128)(2,1)S(1)}, bf16[384,768]{1,0:T(8,128)(2,1)}, bf16[384,1024]{1,0:T(8,128)(2,1)S(1)}, /*index=5*/bf16[384,1024]{1,0:T(8,128)(2,1)}) %tuple.92), branch_computations={%region_6.7_spmd, %region_7.10_spmd} | conditional | flops 756302208 | bytes 9249084 | solution.py:59
  111.7 1.8 fusion.52
  117.7 11.3 %collective-permute-done.10 = bf16[384,768]{1,0:T(8,128)(2,1)} collective-permute-done((bf16[384,768]{1,0:T(8,128)(2,1)S(1)}, bf16[384,768]{1,0:T(8,128)(2,1)}, u32[]{:S(2)}, u32[]{:S(2)}) %collective-permute-start.10) | collective-permute-done | bytes 589856 | tf_op jit(solution)/shard_map/ppermute | solution.py:12
  129.0 7.9 %conditional.8 = (f32[384,768]{1,0:T(8,128)}, f32[]{:T(128)}, f32[]{:T(128)}) conditional(s32[]{:T(128)} %bitcast.3, () %tuple.54, (f32[384]{0:T(512)S(1)}, bf16[384]{0:T(512)(128)(2,1)S(1)}, bf16[384,768]{1,0:T(8,128)(2,1)S(1)}, bf16[384,768]{1,0:T(8,128)(2,1)}, bf16[384,1024]{1,0:T(8,128)(2,1)S(1)}, /*index=5*/bf16[384,1024]{1,0:T(8,128)(2,1)}) %tuple.55), branch_computations={%region_14.15_spmd, %region_15.18_spmd} | conditional | flops 756302208 | bytes 6889760 | solution.py:59
  129.0 1.7 fusion.54
  130.7 2.3 multiply_reduce_fusion.3
  133.0 2.6 fusion.24
  137.0 6.7 %conditional.9 = (f32[384,768]{1,0:T(8,128)S(1)}, f32[]{:T(128)}, f32[]{:T(128)}) conditional(s32[]{:T(128)} %bitcast.4, () %tuple.56, (f32[384]{0:T(512)S(1)}, bf16[384]{0:T(512)(128)(2,1)S(1)}, bf16[384,768]{1,0:T(8,128)(2,1)S(1)}, bf16[384,768]{1,0:T(8,128)(2,1)}, bf16[384,1024]{1,0:T(8,128)(2,1)S(1)}, ...), branch_computations={%region_18.19_spmd, %region_19.22_spmd} | conditional | flops 756302208 | bytes 6889760 | solution.py:59
  137.0 1.7 fusion.55
  138.7 2.2 multiply_reduce_fusion.4
  146.3 110.8 %all-reduce = (f32[]{:T(128)}, f32[]{:T(128)}) all-reduce(f32[]{:T(128)S(6)} %add.79, f32[]{:T(128)S(6)} %add.84), channel_id=1, replica_groups=mesh['group'=8,'member'=64] {'group','member'}, use_global_device_ids=true, to_apply=%region_24.0 | all-reduce | flops 2 | bytes 16 | tf_op jit(solution)/shard_map/psum | solution.py:84
  258.4 3.2 %fusion.39 = (f32[384]{0:T(512)S(1)}, f32[384,768]{1,0:T(8,128)S(1)}) fusion(f32[384,768]{1,0:T(8,128)} %copy-done.3, f32[384,768]{1,0:T(8,128)} %get-tuple-element.110, f32[384,768]{1,0:T(8,128)} %copy-done.2, f32[384,768]{1,0:T(8,128)} %get-tuple-element.108, f32[384,768]{1,0:T(8,128)S(1)} %fusion.45, f32[384,768]{1,0:T(8,128)} %copy-done.1, ...), kind=kLoop, calls=%fused_computation.56 | loop fusion | flops 3243648 | bytes 8850432 | tf_op jit(solution)/shard_map/reduce_sum | solution.py:86
  (63 shorter events, 14.9 us)
Async XLA Ops:
  0.6 1.5 copy-start.4
  0.6 12.4 %copy-start.13 = (s32[384]{0:T(512)S(1)}, s32[384]{0:T(512)}, u32[]{:S(2)}) copy-start(s32[384]{0:T(512)} %param.16) | copy-start | bytes 4612
  0.6 24.2 %copy-start = (bf16[384,768]{1,0:T(8,128)(2,1)S(1)}, bf16[384,768]{1,0:T(8,128)(2,1)}, u32[]{:S(2)}) copy-start(bf16[384,768]{1,0:T(8,128)(2,1)} %param.14) | copy-start | bytes 1769476
  2.3 65.8 %copy-start.14 = (s32[1,1,5]{2,1,0:T(1,128)S(1)}, s32[1,1,5]{2,1,0:T(1,128)}, u32[]{:S(2)}) copy-start(s32[1,1,5]{2,1,0:T(1,128)} %param.17) | copy-start | bytes 64
  2.4 65.8 %collective-permute-start.2 = (bf16[384,1024]{1,0:T(8,128)(2,1)S(1)}, bf16[384,1024]{1,0:T(8,128)(2,1)S(1)}, u32[]{:S(2)}, u32[]{:S(2)}) collective-permute-start(bf16[384,1024]{1,0:T(8,128)(2,1)S(1)} %fusion.36), channel_id=1, source_target_pairs={{0,1},{1,2},{2,3},{3,4},{4,5},{5,6},{6,7},{7,8},{8,9},{9,10},{10,1... | collective-permute-start | bytes 2359304 | tf_op jit(solution)/shard_map/ppermute | solution.py:12
  8.4 86.9 %collective-permute-start.5 = (bf16[384,1024]{1,0:T(8,128)(2,1)S(1)}, bf16[384,1024]{1,0:T(8,128)(2,1)S(1)}, u32[]{:S(2)}, u32[]{:S(2)}) collective-permute-start(bf16[384,1024]{1,0:T(8,128)(2,1)S(1)} %fusion.36), channel_id=1, source_target_pairs={{0,63},{1,0},{2,1},{3,2},{4,3},{5,4},{6,5},{7,6},{8,7},{9,8},{10,9... | collective-permute-start | bytes 2359304 | tf_op jit(solution)/shard_map/ppermute | solution.py:12
  13.1 12.7 %collective-permute-start = (bf16[384]{0:T(512)(128)(2,1)S(1)}, bf16[384]{0:T(512)(128)(2,1)S(1)}, u32[]{:S(2)}, u32[]{:S(2)}) collective-permute-start(bf16[384]{0:T(512)(128)(2,1)S(1)} %get-tuple-element.139), channel_id=1, source_target_pairs={{0,1},{1,2},{2,3},{3,4},{4,5},{5,6},{6,7},{7,8},{8,9},{9,10},{10,1... | collective-permute-start | bytes 2312 | tf_op jit(solution)/shard_map/ppermute | solution.py:12
  15.5 16.2 %collective-permute-start.3 = (bf16[384]{0:T(512)(128)(2,1)S(1)}, bf16[384]{0:T(512)(128)(2,1)S(1)}, u32[]{:S(2)}, u32[]{:S(2)}) collective-permute-start(bf16[384]{0:T(512)(128)(2,1)S(1)} %get-tuple-element.139), channel_id=1, source_target_pairs={{0,63},{1,0},{2,1},{3,2},{4,3},{5,4},{6,5},{7,6},{8,7},{9,8},{10,9... | collective-permute-start | bytes 2312 | tf_op jit(solution)/shard_map/ppermute | solution.py:12
  23.0 16.5 %collective-permute-start.6 = (bf16[384]{0:T(512)(128)(2,1)S(1)}, bf16[384]{0:T(512)(128)(2,1)S(1)}, u32[]{:S(2)}, u32[]{:S(2)}) collective-permute-start(bf16[384]{0:T(512)(128)(2,1)S(1)} %get-tuple-element.139), channel_id=1, source_target_pairs={{0,2},{1,3},{2,4},{3,5},{4,6},{5,7},{6,8},{7,9},{8,10},{9,11},{10,... | collective-permute-start | bytes 2312 | tf_op jit(solution)/shard_map/ppermute | solution.py:12
  25.8 21.1 %collective-permute-start.1 = (bf16[384,768]{1,0:T(8,128)(2,1)S(1)}, bf16[384,768]{1,0:T(8,128)(2,1)S(1)}, u32[]{:S(2)}, u32[]{:S(2)}) collective-permute-start(bf16[384,768]{1,0:T(8,128)(2,1)S(1)} %fusion.38), channel_id=1, source_target_pairs={{0,1},{1,2},{2,3},{3,4},{4,5},{5,6},{6,7},{7,8},{8,9},{9,10},{10,1... | collective-permute-start | bytes 1769480 | tf_op jit(solution)/shard_map/ppermute | solution.py:12
  31.7 13.2 %collective-permute-start.9 = (bf16[384]{0:T(512)(128)(2,1)S(1)}, bf16[384]{0:T(512)(128)(2,1)S(1)}, u32[]{:S(2)}, u32[]{:S(2)}) collective-permute-start(bf16[384]{0:T(512)(128)(2,1)S(1)} %get-tuple-element.139), channel_id=1, source_target_pairs={{0,62},{1,63},{2,0},{3,1},{4,2},{5,3},{6,4},{7,5},{8,6},{9,7},{10,... | collective-permute-start | bytes 2312 | tf_op jit(solution)/shard_map/ppermute | solution.py:12
  39.5 12.7 %collective-permute-start.4 = (bf16[384,768]{1,0:T(8,128)(2,1)S(1)}, bf16[384,768]{1,0:T(8,128)(2,1)S(1)}, u32[]{:S(2)}, u32[]{:S(2)}) collective-permute-start(bf16[384,768]{1,0:T(8,128)(2,1)S(1)} %fusion.38), channel_id=1, source_target_pairs={{0,63},{1,0},{2,1},{3,2},{4,3},{5,4},{6,5},{7,6},{8,7},{9,8},{10,9... | collective-permute-start | bytes 1769480 | tf_op jit(solution)/shard_map/ppermute | solution.py:12
  44.9 20.1 %collective-permute-start.7 = (bf16[384,768]{1,0:T(8,128)(2,1)S(1)}, bf16[384,768]{1,0:T(8,128)(2,1)S(1)}, u32[]{:S(2)}, u32[]{:S(2)}) collective-permute-start(bf16[384,768]{1,0:T(8,128)(2,1)S(1)} %fusion.38), channel_id=1, source_target_pairs={{0,2},{1,3},{2,4},{3,5},{4,6},{5,7},{6,8},{7,9},{8,10},{9,11},{10,... | collective-permute-start | bytes 1769480 | tf_op jit(solution)/shard_map/ppermute | solution.py:12
  46.8 18.2 %copy-start.9 = (bf16[384,768]{1,0:T(8,128)(2,1)}, bf16[384,768]{1,0:T(8,128)(2,1)S(1)}, u32[]{:S(2)}) copy-start(bf16[384,768]{1,0:T(8,128)(2,1)S(1)} %collective-permute-done.1) | copy-start | bytes 1769476
  46.9 62.9 %collective-permute-start.8 = (bf16[384,1024]{1,0:T(8,128)(2,1)S(1)}, bf16[384,1024]{1,0:T(8,128)(2,1)}, u32[]{:S(2)}, u32[]{:S(2)}) collective-permute-start(bf16[384,1024]{1,0:T(8,128)(2,1)S(1)} %fusion.36), channel_id=1, source_target_pairs={{0,2},{1,3},{2,4},{3,5},{4,6},{5,7},{6,8},{7,9},{8,10},{9,11},{10,... | collective-permute-start | bytes 2359304 | tf_op jit(solution)/shard_map/ppermute | solution.py:12
  52.2 12.9 %copy-start.7 = (bf16[384,768]{1,0:T(8,128)(2,1)}, bf16[384,768]{1,0:T(8,128)(2,1)S(1)}, u32[]{:S(2)}) copy-start(bf16[384,768]{1,0:T(8,128)(2,1)S(1)} %collective-permute-done.4) | copy-start | bytes 1769476
  52.2 76.8 %collective-permute-start.11 = (bf16[384,1024]{1,0:T(8,128)(2,1)S(1)}, bf16[384,1024]{1,0:T(8,128)(2,1)}, u32[]{:S(2)}, u32[]{:S(2)}) collective-permute-start(bf16[384,1024]{1,0:T(8,128)(2,1)S(1)} %fusion.36), channel_id=1, source_target_pairs={{0,62},{1,63},{2,0},{3,1},{4,2},{5,3},{6,4},{7,5},{8,6},{9,7},{10,... | collective-permute-start | bytes 2359304 | tf_op jit(solution)/shard_map/ppermute | solution.py:12
  65.0 0.8 copy-start.5
  65.9 71.1 %collective-permute-start.14 = (bf16[384,1024]{1,0:T(8,128)(2,1)S(1)}, bf16[384,1024]{1,0:T(8,128)(2,1)}, u32[]{:S(2)}, u32[]{:S(2)}) collective-permute-start(bf16[384,1024]{1,0:T(8,128)(2,1)S(1)} %fusion.36), channel_id=1, source_target_pairs={{0,64},{64,0},{128,192},{192,128},{256,320},{320,256},{384,448},{4... | collective-permute-start | bytes 2359304 | tf_op jit(solution)/shard_map/ppermute | solution.py:22
  68.1 60.8 %collective-permute-start.10 = (bf16[384,768]{1,0:T(8,128)(2,1)S(1)}, bf16[384,768]{1,0:T(8,128)(2,1)}, u32[]{:S(2)}, u32[]{:S(2)}) collective-permute-start(bf16[384,768]{1,0:T(8,128)(2,1)S(1)} %fusion.38), channel_id=1, source_target_pairs={{0,62},{1,63},{2,0},{3,1},{4,2},{5,3},{6,4},{7,5},{8,6},{9,7},{10,... | collective-permute-start | bytes 1769480 | tf_op jit(solution)/shard_map/ppermute | solution.py:12
  95.3 5.8 %copy-start.11 = (bf16[384,1024]{1,0:T(8,128)(2,1)}, bf16[384,1024]{1,0:T(8,128)(2,1)S(1)}, u32[]{:S(2)}) copy-start(bf16[384,1024]{1,0:T(8,128)(2,1)S(1)} %collective-permute-done.5) | copy-start | bytes 2359300
  95.3 41.6 %collective-permute-start.13 = (bf16[384,768]{1,0:T(8,128)(2,1)S(1)}, bf16[384,768]{1,0:T(8,128)(2,1)}, u32[]{:S(2)}, u32[]{:S(2)}) collective-permute-start(bf16[384,768]{1,0:T(8,128)(2,1)S(1)} %fusion.38), channel_id=1, source_target_pairs={{0,64},{64,0},{128,192},{192,128},{256,320},{320,256},{384,448},{4... | collective-permute-start | bytes 1769480 | tf_op jit(solution)/shard_map/ppermute | solution.py:22
  103.7 0.9 copy-start.12
  103.7 2.6 copy-start.10
  109.1 2.6 copy-start.1
  109.8 27.2 %collective-permute-start.12 = (bf16[384]{0:T(512)(128)(2,1)S(1)}, bf16[384]{0:T(512)(128)(2,1)S(1)}, u32[]{:S(2)}, u32[]{:S(2)}) collective-permute-start(bf16[384]{0:T(512)(128)(2,1)S(1)} %get-tuple-element.139), channel_id=1, source_target_pairs={{0,64},{64,0},{128,192},{192,128},{256,320},{320,256},{384,448},{4... | collective-permute-start | bytes 2312 | tf_op jit(solution)/shard_map/ppermute | solution.py:22
  111.7 1.8 copy-start.8
  117.7 11.3 %copy-start.2 = (f32[384,768]{1,0:T(8,128)}, f32[384,768]{1,0:T(8,128)S(1)}, u32[]{:S(2)}) copy-start(f32[384,768]{1,0:T(8,128)S(1)} %get-tuple-element.109) | copy-start | bytes 3538948
  143.7 1.0 copy-start.3
where the time goes:
time: 265 us; the launch traced here: 264 us
  blocking collectives  111 us (42%)
  starting transfers between devices  88.8 us (34%)
  matrix products  24.1 us (9%)
  waiting for transfers between devices  17.9 us (7%)
  between operations  7.98 us (3%)
  other arithmetic  6.54 us (2%)
  loops' own time  5.08 us (2%)
  local copies, waits for them, and re-layouts  2.83 us (1%)
    psum x1, blocking collectives, per_device(): loss_sum, weight_sum = lax.psum((loss_sum, weight_sum), ('group', 'member'))  111 us
    ppermute x12, starting transfers between devices, passed_along(): return lax.ppermute(value, axis, pairs)  82.7 us
    ppermute x12, waiting for transfers between devices, passed_along(): return lax.ppermute(value, axis, pairs)  17.9 us
    dot_general x5, matrix products, compute(): jnp.einsum('id,jd->ij', local_s, partner_s, preferred_element_type=jnp.fl...  8.76 us
    dot_general x5, matrix products, compute(): jnp.dot(coefficient, partner_s, preferred_element_type=jnp.float32)  7.82 us
    dot_general x5, matrix products, compute(): jnp.einsum('id,jd->ij', local_t, partner_t, preferred_element_type=jnp.fl...  7.53 us
    ppermute x3, starting transfers between devices, partner_2(): return lax.ppermute(block, axis, route)  6.05 us
  transfers between devices with their start and end apart: 15, of which 4 were waited for; matrix products, arithmetic and copies ran while one was open for 7% of the time, Pallas kernels for 0%

commit v1 on v0

v1 whole, which is shorter than its diff:
```python
import functools

import jax
import jax.numpy as jnp
from jax import lax
from jax.experimental import pallas as pl
from jax.experimental.pallas import tpu as pltpu
from jax.sharding import PartitionSpec as P

EPS = 1e-06
MESH = pl.DeviceIdType.MESH
ROWS = 384
DS = 768
DT = 1024
DU = DS + DT
THIRD = 128
CHUNK = 32
NC = ROWS // CHUNK
F32 = jnp.float32
BF16 = jnp.bfloat16


def kernel(
    n_group, n_member,
    s_hbm, t_hbm, c_ref, plan_ref,
    grad_hbm, loss_ref,
    s_in, t_in, slots, lhs, acc, scale, wcol, wbuf, wrow, lossacc, tiles, out_buf,
    in_sem, send, recv, xsend, xrecv, wsend, wrecv, ar_send, ar_recv, out_sem,
):
    g = lax.axis_index("group")
    m = lax.axis_index("member")
    core = lax.rem(m, 2)
    x_hi = lax.rem(m // 2, 2)
    g_xor = g + 1 - 2 * lax.rem(g, 2)
    m_core = m + 1 - 2 * core
    m_xhi = m + 2 - 4 * x_hi
    m_z = lax.rem(m + 4 - 8 * x_hi + n_member, n_member)
    m_zback = lax.rem(m - 4 + 8 * x_hi + n_member, n_member)
    m_r = lax.rem(m - 2 + 4 * x_hi + n_member, n_member)
    m_f = lax.rem(m - 1 + 2 * core + n_member, n_member)

    def device(group, member):
        return {"group": group, "member": member}

    def rounds(r, d):
        if r == 0:
            base = (m // 8) * 8
            return device(g, base + lax.rem(m - base + d, 8))
        if r == 1:
            return device(lax.rem(g + d, 8), m)
        return device(g, lax.rem(m + 8 * d, n_member))

    copies = []
    for third in range(3):
        rows = pl.ds(third * THIRD, THIRD)
        for which, (src, dst) in enumerate(((s_hbm, s_in), (t_hbm, t_in))):
            copy = pltpu.make_async_copy(src.at[rows], dst.at[rows], in_sem.at[which, third])
            copy.start()
            copies.append(copy)

    barrier = pltpu.get_barrier_semaphore()
    peers = [
        device(g, m_core), device(g_xor, m), device(g, m_xhi), device(g, m_r), device(g, m_f),
        device(g_xor, m_xhi), device(g, m_z), device(g, m_zback),
    ]
    for r in range(3):
        for d in range(1, 8):
            peers.append(rounds(r, d))
    for peer in peers:
        pl.semaphore_signal(barrier, inc=1, device_id=peer, device_id_type=MESH)

    for third in range(3):
        row = c_ref[:, third * THIRD:(third + 1) * THIRD].astype(F32)
        wide = jnp.broadcast_to(row, (THIRD, THIRD))
        wcol[pl.ds(third * THIRD, THIRD), :] = wide.T
        wbuf[0, third] = jnp.broadcast_to(row, (8, THIRD))

    def normalise(k):
        rows = pl.ds(pl.multiple_of(k * CHUNK, CHUNK), CHUNK)
        x = s_in[rows, :].astype(F32)
        rs = lax.rsqrt(jnp.sum(x * x, axis=-1, keepdims=True) + EPS)
        u = (x * rs).astype(BF16)
        slots[0, rows, 0:DS] = u
        lhs[rows, 0:DS] = u
        scale[rows, :] = rs
        y = t_in[rows, :].astype(F32)
        ts = lax.rsqrt(jnp.sum(y * y, axis=-1, keepdims=True) + EPS)
        v = (y * ts).astype(BF16)
        slots[0, rows, DS:DU] = v
        lhs[rows, DS:DU] = -v

    def block_copy(k, src, dst, flow, to):
        rows = pl.ds(pl.multiple_of(k * CHUNK, CHUNK), CHUNK)
        return pltpu.make_async_remote_copy(
            src_ref=slots.at[src, rows], dst_ref=slots.at[dst, rows],
            send_sem=send.at[flow, k], recv_sem=recv.at[flow, k],
            device_id=to, device_id_type=MESH,
        )

    to_p = lambda k: block_copy(k, 0, 2, 0, device(g_xor, m))
    to_q = lambda k: block_copy(k, 2, 3, 1, device(g_xor, m_xhi))
    to_r = lambda k: block_copy(k, 3, 4, 2, device(g, m_z))
    role = lax.rem(x_hi + core, 2)
    to_f = lambda k: block_copy(k, 3 + role, 5, 3, device(g, m_core))

    def to_core(third):
        rows = pl.ds(pl.multiple_of(third * THIRD, THIRD), THIRD)
        return pltpu.make_async_remote_copy(
            src_ref=slots.at[0, rows], dst_ref=slots.at[1, rows],
            send_sem=xsend.at[third], recv_sem=xrecv.at[third],
            device_id=device(g, m_core), device_id_type=MESH,
        )

    per_third = THIRD // CHUNK
    w_peers = [device(g, m_core), device(g_xor, m), device(g, m_xhi), device(g, m_r), device(g, m_f)]
    w_copies = [
        pltpu.make_async_remote_copy(
            src_ref=wbuf.at[0], dst_ref=wbuf.at[slot + 1],
            send_sem=wsend.at[slot], recv_sem=wrecv.at[slot],
            device_id=peer, device_id_type=MESH,
        )
        for slot, peer in enumerate(w_peers)
    ]

    for third in range(3):
        copies[2 * third].wait()
        copies[2 * third + 1].wait()

        @pl.loop(third * per_third, (third + 1) * per_third)
        def _(k):
            normalise(k)

        if third == 0:
            pl.semaphore_wait(barrier, len(peers))

        @pl.loop(third * per_third, (third + 1) * per_third)
        def _(k):
            to_p(k).start()

        to_core(third).start()
        if third == 0:
            for copy in w_copies:
                copy.start()

    acc[...] = jnp.zeros_like(acc)
    lossacc[...] = jnp.zeros_like(lossacc)

    low, high = 0, 2
    columns = [high - 2 * core, 4 + 0 * core, 3 - 2 * x_hi, 1 + 2 * x_hi, 2 * core]
    total_w = jnp.zeros((8, THIRD), F32)
    for third in range(3):
        wrow[0, third] = wbuf[0, third]
        total_w = total_w + wbuf[0, third]
    own_w = jnp.sum(total_w, axis=-1, keepdims=True)
    for slot in range(5):
        w_copies[slot].wait()
        switch = plan_ref[0, 0, columns[slot]].astype(F32)
        for third in range(3):
            w = wbuf[slot + 1, third] * switch
            wrow[slot + 1, third] = w
            total_w = total_w + w
    weight_lanes = total_w * own_w

    def piece(pair, third):
        rows = pl.ds(pl.multiple_of(third * THIRD, THIRD), THIRD)
        both = jnp.concatenate([slots[2 * pair, rows, :], slots[2 * pair + 1, rows, :]], axis=0)
        diff = lax.dot_general(
            lhs[...], both, (((1,), (1,)), ((), ())), preferred_element_type=F32
        )
        w_j = jnp.concatenate([wrow[2 * pair, third], wrow[2 * pair + 1, third]], axis=1)[0:1]
        w_i = wcol[...]
        weighted = jnp.concatenate([w_i, w_i], axis=1) * w_j * diff
        loss = weighted * diff
        lossacc[...] += jnp.sum(loss.reshape(ROWS // 8, 8, 2 * THIRD), axis=0)
        acc[...] += jnp.dot(weighted.astype(BF16), both[:, 0:DS], preferred_element_type=F32)

    @pl.loop(0, NC + 3)
    def _(k):
        @pl.when(k < NC)
        def _():
            to_p(k).wait_recv()
            to_q(k).start()

        @pl.when((k >= 1) & (k <= NC))
        def _():
            to_q(k - 1).wait_recv()
            to_r(k - 1).start()

        @pl.when((k >= 2) & (k <= NC + 1))
        def _():
            to_r(k - 2).wait_recv()
            to_f(k - 2).start()

        @pl.when(k >= 3)
        def _():
            to_f(k - 3).wait_recv()

        @pl.when(k < 3)
        def _():
            to_core(k).wait_recv()

        @pl.when((k < 3) | (lax.rem(k, 2) == 0))
        def _():
            early = jnp.where(k < 3, 1, 0)
            q = jnp.maximum(k - 4, 0)
            pair = (1 - early) * (1 + lax.rem(q // 2, 2))
            third = early * k + (1 - early) * (q // 4)
            piece(pair, third)

    loss_lanes = jnp.sum(lossacc[:, 0:THIRD] + lossacc[:, THIRD:], axis=0, keepdims=True)
    row_id = lax.broadcasted_iota(jnp.int32, (8, THIRD), 0)
    tile = jnp.where(row_id == 0, jnp.broadcast_to(loss_lanes, (8, THIRD)), weight_lanes)
    place = [lax.rem(m, 8), g, m // 8]

    def send_round(r, value):
        tiles[r, place[r]] = value
        for d in range(1, 8):
            pltpu.make_async_remote_copy(
                src_ref=tiles.at[r, place[r]], dst_ref=tiles.at[r, place[r]],
                send_sem=ar_send.at[r], recv_sem=ar_recv.at[r],
                device_id=rounds(r, d), device_id_type=MESH,
            ).start()

    def finish_round(r):
        seven = tiles.at[r, pl.ds(0, 7)]
        pltpu.make_async_copy(seven, seven, ar_recv.at[r]).wait()
        total = tiles[r, 0]
        for d in range(1, 8):
            total = total + tiles[r, d]
        return total

    send_round(0, tile)

    @pl.loop(0, NC)
    def _(k):
        rows = pl.ds(pl.multiple_of(k * CHUNK, CHUNK), CHUNK)
        u = slots[0, rows, 0:DS].astype(F32)
        a = acc[rows, :]
        along = jnp.sum(a * u, axis=-1, keepdims=True)
        out_buf[rows, :] = (4.0 * scale[rows, :]) * (a - along * u)

    out_copy = pltpu.make_async_copy(out_buf, grad_hbm, out_sem)
    out_copy.start()

    tile = finish_round(0)
    send_round(1, tile)
    tile = finish_round(1)
    send_round(2, tile)

    @pl.loop(0, NC)
    def _(k):
        for copy in (to_p, to_q, to_r, to_f):
            copy(k).wait_send()

    for third in range(3):
        to_core(third).wait_send()

    tile = finish_round(2)
    sums = jnp.sum(tile, axis=-1, keepdims=True)
    loss_ref[...] = DS * sums[0:1] / sums[1:2]

    for r in range(3):
        seven = tiles.at[r, pl.ds(0, 7)]
        pltpu.make_async_copy(seven, seven, ar_send.at[r]).wait()
    out_copy.wait()


def per_device(student, teacher, counts, plan):
    n_group = lax.axis_size("group")
    n_member = lax.axis_size("member")
    any_space = pl.BlockSpec(memory_space=pl.ANY)
    vmem = pl.BlockSpec(memory_space=pltpu.VMEM)
    smem = pl.BlockSpec(memory_space=pltpu.SMEM)
    dma = pltpu.SemaphoreType.DMA
    grad, loss = pl.pallas_call(
        functools.partial(kernel, n_group, n_member),
        out_shape=(
            jax.ShapeDtypeStruct((ROWS, DS), F32),
            jax.ShapeDtypeStruct((1, 1), F32),
        ),
        in_specs=[any_space, any_space, vmem, smem],
        out_specs=(any_space, vmem),
        scratch_shapes=[
            pltpu.VMEM((ROWS, DS), BF16),
            pltpu.VMEM((ROWS, DT), BF16),
            pltpu.VMEM((6, ROWS, DU), BF16),
            pltpu.VMEM((ROWS, DU), BF16),
            pltpu.VMEM((ROWS, DS), F32),
            pltpu.VMEM((ROWS, 1), F32),
            pltpu.VMEM((ROWS, THIRD), F32),
            pltpu.VMEM((6, 3, 8, THIRD), F32),
            pltpu.VMEM((6, 3, 8, THIRD), F32),
            pltpu.VMEM((8, 2 * THIRD), F32),
            pltpu.VMEM((3, 8, 8, THIRD), F32),
            pltpu.VMEM((ROWS, DS), F32),
            dma((2, 3)),
            dma((4, NC)),
            dma((4, NC)),
            dma((3,)),
            dma((3,)),
            dma((5,)),
            dma((5,)),
            dma((3,)),
            dma((3,)),
            dma,
        ],
        compiler_params=pltpu.CompilerParams(
            collective_id=0, has_side_effects=True, vmem_limit_bytes=48 * 1024 * 1024
        ),
    )(student, teacher, counts.reshape(1, ROWS), plan)
    return grad, loss.reshape(())


def solution(mesh):
    return jax.shard_map(
        per_device,
        mesh=mesh,
        in_specs=(
            P(("group", "member"), None),
            P(("group", "member"), None),
            P(("group", "member")),
            P("group", "member", None),
        ),
        out_specs=(P(("group", "member"), None), P()),
        check_vma=False,
    )
```

time: 265 us -> 102 us (0.38)
  blocking collectives: 111 us -> 0 us
  Pallas kernels: 0 us -> 94.4 us
  starting transfers between devices: 88.8 us -> 0 us
  matrix products: 24.1 us -> 0 us
  waiting for transfers between devices: 17.9 us -> 0 us
  other arithmetic: 6.54 us -> 0 us
  between operations: 7.98 us -> 2.38 us
  loops' own time: 5.08 us -> 0 us
    psum x1 -> x0, blocking collectives: 111 us -> none  [per_device(): loss_sum, weight_sum = lax.psum((loss_sum, weight_sum), ('group', 'member'))]
    pallas_call x0 -> x1, Pallas kernels: none -> 94.4 us  [per_device(): pl.pallas_call(functools.partial(kernel, n_group, n_member), out_shape=(j...]
    ppermute x15 -> x0, starting transfers between devices: 88.8 us -> none  [the longest x12 82.7 us: passed_along(): return lax.ppermute(value, axis, pairs)]
    dot_general x15 -> x0, matrix products: 24.1 us -> none  [the longest x5 8.76 us: compute(): jnp.einsum('id,jd->ij', local_s, partner_s, preferred_element_type=jnp.fl...]
    ppermute x15 -> x0, waiting for transfers between devices: 17.9 us -> none  [the longest x12 17.9 us: passed_along(): return lax.ppermute(value, axis, pairs)]
    another operation x5 -> x0, loops' own time: 5.08 us -> none  [block_terms(): return lax.cond(switch > 0, compute, skipped, 0)]
    reduce_sum x3 -> x0, other arithmetic: 4.84 us -> none  [the longest x1 3.17 us: per_device(): along_unit = jnp.sum(summed_grad * unit_float, axis=-1, keepdims=True)]
    unnamed x22 -> x7, local copies, waits for them, and re-layouts: 1.2 us -> 3.87 us
  transfers between devices with their start and end apart: 15 -> 0, of which waited for: 4 -> 0; matrix products, arithmetic and copies ran while one was open for 7% -> 0% of each run, Pallas kernels for 0% -> 0%
where the time goes in v1:
time: 102 us; the launch traced here: 101 us
  Pallas kernels  94.4 us (93%)
  local copies, waits for them, and re-layouts  4.55 us (4%)
  between operations  2.38 us (2%)
    pallas_call x1, Pallas kernels, per_device(): pl.pallas_call(functools.partial(kernel, n_group, n_member), out_shape=(j...  94.4 us
    unnamed x7, local copies, waits for them, and re-layouts  3.87 us

profile of v1, /device:TPU:1, one launch (start us, length us, event | category | flops | bytes accessed | tf_op | source)
XLA Modules:
  0.0 101.4 jit_solution(11479156301861339218)
XLA Ops:
  0.6 0.7 reshape.10.c_ref
  1.3 0.0 copy-start
  1.3 1.1 %copy-done = bf16[384,1024]{1,0:T(8,128)(2,1)S(1)} copy-done((bf16[384,1024]{1,0:T(8,128)(2,1)S(1)}, bf16[384,1024]{1,0:T(8,128)(2,1)}, u32[]{:S(2)}) %copy-start) | copy-done | bytes 786456
  2.4 0.0 copy-start.1
  2.4 1.1 %copy-done.1 = bf16[384,768]{1,0:T(8,128)(2,1)S(1)} copy-done((bf16[384,768]{1,0:T(8,128)(2,1)S(1)}, bf16[384,768]{1,0:T(8,128)(2,1)}, u32[]{:S(2)}) %copy-start.1) | copy-done | bytes 589848
  3.5 0.0 copy-start.2
  3.5 0.7 copy-done.2
  4.2 94.4 %shard_map.59 = (f32[384,768]{1,0:T(8,128)S(1)}, f32[1,1]{1,0:T(1,128)}) custom-call(bf16[384,768]{1,0:T(8,128)(2,1)S(1)} %copy-done.1, bf16[384,1024]{1,0:T(8,128)(2,1)S(1)} %copy-done, s32[1,384]{1,0:T(1,128)S(1)} %reshape.10.c_ref, s32[1,1,5]{2,1,0:T(1,128)S(1)} %copy-done.2), custom_call_target="tpu_custom_call" | custom-call | tf_op jit(solution)/shard_map/pallas_call | solution.py:275
  98.6 1.0 %copy.8 = f32[384,768]{1,0:T(8,128)} copy(f32[384,768]{1,0:T(8,128)S(1)} %get-tuple-element.8) | data formatting | bytes 2359296
Async XLA Ops:
  1.3 1.1 %copy-start = (bf16[384,1024]{1,0:T(8,128)(2,1)S(1)}, bf16[384,1024]{1,0:T(8,128)(2,1)}, u32[]{:S(2)}) copy-start(bf16[384,1024]{1,0:T(8,128)(2,1)} %t_hbm.1) | copy-start | bytes 2359300
  2.4 1.1 %copy-start.1 = (bf16[384,768]{1,0:T(8,128)(2,1)S(1)}, bf16[384,768]{1,0:T(8,128)(2,1)}, u32[]{:S(2)}) copy-start(bf16[384,768]{1,0:T(8,128)(2,1)} %s_hbm.1) | copy-start | bytes 1769476
  3.5 0.7 copy-start.2

commit v2 on v1

v2 whole, which is shorter than its diff:
```python
import functools
import itertools

import jax
import jax.numpy as jnp
from jax import lax
from jax.experimental import pallas as pl
from jax.experimental.pallas import tpu as pltpu
from jax.sharding import PartitionSpec as P

EPS = 1e-06
MESH = pl.DeviceIdType.MESH
ROWS = 384
DS = 768
DT = 1024
DU = DS + DT
THIRD = 128
CHUNK = 16
NC = ROWS // CHUNK
PER_THIRD = NC // 3
LAG_Q, LAG_R, LAG_F = 3, 6, 8
STEPS = NC + LAG_F
EARLY = 3
TOKENS = 8
NORM = 32
F32 = jnp.float32
BF16 = jnp.bfloat16


def kernel(
    n_group, n_member,
    s_hbm, t_hbm, c_hbm, plan_hbm,
    grad_hbm, loss_ref,
    s_in, t_in, c_in, plan_in, switches, slots, lhs, acc, scale, wcol, wbuf, lossacc, tiles, out_buf,
    in_sem, send, recv, xsend, xrecv, wsend, wrecv, ar_send, ar_recv, out_sem, tokens,
):
    g = lax.axis_index("group")
    m = lax.axis_index("member")
    core = lax.rem(m, 2)
    x_hi = lax.rem(m // 2, 2)
    x_lo = lax.rem(g, 2)
    g_xor = g + 1 - 2 * x_lo
    m_core = m + 1 - 2 * core
    m_xhi = m + 2 - 4 * x_hi
    m_up = lax.rem(m + 4, n_member)
    m_down = lax.rem(m - 4 + n_member, n_member)
    m_z = lax.rem(m + 4 - 8 * x_hi + n_member, n_member)
    g_up = lax.rem(g + 2, n_group)
    g_down = lax.rem(g - 2 + n_group, n_group)
    role = lax.rem(x_hi + core, 2)

    def device(group, member):
        return {"group": group, "member": member}

    small = [
        pltpu.make_async_copy(c_hbm, c_in, in_sem.at[2, 0]),
        pltpu.make_async_copy(plan_hbm, plan_in, in_sem.at[2, 1]),
    ]
    copies = []
    for third in range(3):
        rows = pl.ds(third * THIRD, THIRD)
        for which, (src, dst) in enumerate(((s_hbm, s_in), (t_hbm, t_in))):
            copies.append(pltpu.make_async_copy(src.at[rows], dst.at[rows], in_sem.at[which, third]))
    for copy in copies[:2] + small + copies[2:]:
        copy.start()

    barrier = pltpu.get_barrier_semaphore()
    xor_peer = device(g_xor, m)
    x_other = device(g_xor, m_xhi)
    sides = [
        (xor_peer, 0), (x_other, 1),
        (device(g, m_up), 3), (device(g, m_down), 2),
        (device(g_up, m), 5), (device(g_down, m), 4),
    ]
    near = [peer for peer, _ in sides] + [device(g, m_core)]
    for peer in near:
        pl.semaphore_signal(barrier, inc=1, device_id=peer, device_id_type=MESH)

    def normalise(k):
        rows = pl.ds(pl.multiple_of(k * NORM, NORM), NORM)
        x = s_in[rows, :].astype(F32)
        rs = lax.rsqrt(jnp.sum(x * x, axis=-1, keepdims=True) + EPS)
        u = (x * rs).astype(BF16)
        slots[0, rows, 0:DS] = u
        lhs[rows, 0:DS] = u
        scale[rows, :] = rs
        y = t_in[rows, :].astype(F32)
        ts = lax.rsqrt(jnp.sum(y * y, axis=-1, keepdims=True) + EPS)
        v = (y * ts).astype(BF16)
        slots[0, rows, DS:DU] = v
        lhs[rows, DS:DU] = -v

    flows = [
        (0, 2, xor_peer), (2, 3, x_other), (3, 4, device(g, m_z)), (3 + role, 5, device(g, m_core)),
    ]

    def block_copy(flow, k):
        src, dst, to = flows[flow]
        rows = pl.ds(pl.multiple_of(k * CHUNK, CHUNK), CHUNK)
        return pltpu.make_async_remote_copy(
            src_ref=slots.at[src, rows], dst_ref=slots.at[dst, rows],
            send_sem=send.at[flow, k], recv_sem=recv.at[flow, k],
            device_id=to, device_id_type=MESH,
        )

    def w_copy(flow):
        src, dst, to = (flows + [(0, 1, device(g, m_core))])[flow]
        return pltpu.make_async_remote_copy(
            src_ref=wbuf.at[src], dst_ref=wbuf.at[dst],
            send_sem=wsend.at[flow], recv_sem=wrecv.at[flow],
            device_id=to, device_id_type=MESH,
        )

    def to_core(third):
        rows = pl.ds(pl.multiple_of(third * THIRD, THIRD), THIRD)
        return pltpu.make_async_remote_copy(
            src_ref=slots.at[0, rows], dst_ref=slots.at[1, rows],
            send_sem=xsend.at[third], recv_sem=xrecv.at[third],
            device_id=device(g, m_core), device_id_type=MESH,
        )

    for third in range(3):
        copies[2 * third].wait()
        copies[2 * third + 1].wait()

        @pl.loop(third * (THIRD // NORM), (third + 1) * (THIRD // NORM))
        def _(k):
            normalise(k)

        if third == 0:
            for copy in small:
                copy.wait()
            for part in range(3):
                row = c_in[pl.ds(part * THIRD, THIRD)].astype(F32).reshape(1, THIRD)
                wide = jnp.broadcast_to(row, (THIRD, THIRD))
                wcol[pl.ds(part * THIRD, THIRD), :] = wide.T
                wbuf[0, part] = jnp.broadcast_to(row, (8, THIRD))
            pl.semaphore_wait(barrier, len(near))

        @pl.loop(third * PER_THIRD, (third + 1) * PER_THIRD)
        def _(k):
            block_copy(0, k).start()

        to_core(third).start()
        if third == 0:
            w_copy(0).start()
            w_copy(4).start()

    acc[...] = jnp.zeros_like(acc)
    lossacc[...] = jnp.zeros_like(lossacc)

    columns = [2 - 2 * core, 4 + 0 * core, 3 - 2 * x_hi, 1 + 2 * x_hi, 2 * core]
    switches[0] = jnp.float32(1.0)
    for slot in range(5):
        switches[slot + 1] = plan_in[0, 0, columns[slot]].astype(F32)
    w_copy(4).wait_recv()

    def piece(pair, third):
        rows = pl.ds(pl.multiple_of(third * THIRD, THIRD), THIRD)
        both = jnp.concatenate([slots[2 * pair, rows, :], slots[2 * pair + 1, rows, :]], axis=0)
        diff = lax.dot_general(
            lhs[...], both, (((1,), (1,)), ((), ())), preferred_element_type=F32
        )
        w_j = jnp.concatenate(
            [wbuf[2 * pair + b, third] * switches[2 * pair + b] for b in range(2)], axis=1
        )[0:1]
        w_i = wcol[...]
        weighted = jnp.concatenate([w_i, w_i], axis=1) * w_j * diff
        loss = weighted * diff
        lossacc[...] += jnp.sum(loss.reshape(ROWS // 8, 8, 2 * THIRD), axis=0)
        acc[...] += jnp.dot(weighted.astype(BF16), both[:, 0:DS], preferred_element_type=F32)

    def signal_sides():
        for peer, place in sides:
            pl.semaphore_signal(tokens.at[place], inc=1, device_id=peer, device_id_type=MESH)

    def wait_sides():
        for place in range(6):
            pl.semaphore_wait(tokens.at[place], 1)

    @pl.loop(0, STEPS)
    def _(k):
        @pl.when(k < NC)
        def _():
            block_copy(0, k).wait_recv()
            block_copy(1, k).start()

        for flow, lag in ((1, LAG_Q), (2, LAG_R)):
            @pl.when((k >= lag) & (k < NC + lag))
            def _():
                block_copy(flow, k - lag).wait_recv()
                block_copy(flow + 1, k - lag).start()

        @pl.when(k >= LAG_F)
        def _():
            block_copy(3, k - LAG_F).wait_recv()

        for flow, lag in enumerate((0, LAG_Q, LAG_R, LAG_F)):
            @pl.when(k == lag)
            def _():
                w_copy(flow).wait_recv()
                if flow < 3:
                    w_copy(flow + 1).start()

        @pl.when((k >= 2) & (k < 2 + TOKENS))
        def _():
            signal_sides()

        @pl.when((k >= 4) & (k < 4 + TOKENS))
        def _():
            wait_sides()

        @pl.when((k < 2 * EARLY) & (lax.rem(k, 2) == 0))
        def _():
            to_core(k // 2).wait_recv()
            piece(0, k // 2)

        ready = (LAG_Q + PER_THIRD - 1, LAG_F + PER_THIRD - 1)
        for pair in range(2):
            late = k - ready[pair]

            @pl.when((late >= 0) & (lax.rem(late + 3 * NC, PER_THIRD) == 0) & (late < NC))
            def _():
                piece(1 + pair, late // PER_THIRD)

    total_w = jnp.zeros((8, THIRD), F32)
    own_w = jnp.zeros((8, THIRD), F32)
    for third in range(3):
        own_w = own_w + wbuf[0, third]
        for slot in range(6):
            total_w = total_w + wbuf[slot, third] * switches[slot]
    weight_lanes = total_w * jnp.sum(own_w, axis=-1, keepdims=True)
    loss_lanes = jnp.sum(lossacc[:, 0:THIRD] + lossacc[:, THIRD:], axis=0, keepdims=True)
    row_id = lax.broadcasted_iota(jnp.int32, (8, THIRD), 0)
    tile = jnp.where(row_id == 0, jnp.broadcast_to(loss_lanes, (8, THIRD)), weight_lanes)

    y = g // 2
    z = m // 4
    n_y, n_z = n_group // 2, n_member // 4

    def plane_peer(dh, dl, dy):
        member = m + 2 * (lax.rem(x_hi + dh, 2) - x_hi)
        group = g + (lax.rem(x_lo + dl, 2) - x_lo) + 2 * (lax.rem(y + dy, n_y) - y)
        return device(group, member)

    def around(d, n):
        return min(d, n - d)

    plane = sorted(
        (o for o in itertools.product(range(2), range(2), range(n_y)) if any(o)),
        key=lambda o: (-(2 * o[0] + o[1] - 2 * o[0] * o[1] + around(o[2], n_y)), o),
    )
    ring = sorted(range(1, n_z), key=lambda d: (-around(d, n_z), d))
    rounds = [
        (core, [device(g, m_core)]),
        ((x_hi * 2 + x_lo) * n_y + y, [plane_peer(*o) for o in plane]),
        (z, [device(g, lax.rem(m + 4 * d, n_member)) for d in ring]),
    ]

    def send_round(r, value):
        place, peers = rounds[r]
        tiles[r, place] = value
        for peer in peers:
            pltpu.make_async_remote_copy(
                src_ref=tiles.at[r, place], dst_ref=tiles.at[r, place],
                send_sem=ar_send.at[r], recv_sem=ar_recv.at[r],
                device_id=peer, device_id_type=MESH,
            ).start()

    def all_of(r, sems):
        seen = tiles.at[r, pl.ds(0, len(rounds[r][1]))]
        return pltpu.make_async_copy(seen, seen, sems.at[r])

    def finish_round(r):
        all_of(r, ar_recv).wait()
        total = tiles[r, 0]
        for d in range(1, len(rounds[r][1]) + 1):
            total = total + tiles[r, d]
        return total

    send_round(0, tile)
    tile = finish_round(0)
    send_round(1, tile)

    @pl.loop(0, ROWS // NORM)
    def _(k):
        rows = pl.ds(pl.multiple_of(k * NORM, NORM), NORM)
        u = slots[0, rows, 0:DS].astype(F32)
        a = acc[rows, :]
        along = jnp.sum(a * u, axis=-1, keepdims=True)
        out_buf[rows, :] = (4.0 * scale[rows, :]) * (a - along * u)

    out_copy = pltpu.make_async_copy(out_buf, grad_hbm, out_sem)
    out_copy.start()

    tile = finish_round(1)
    send_round(2, tile)

    @pl.loop(0, NC)
    def _(k):
        for flow in range(4):
            block_copy(flow, k).wait_send()

    for third in range(3):
        to_core(third).wait_send()
    for flow in range(5):
        w_copy(flow).wait_send()
    for r in range(2):
        all_of(r, ar_send).wait()
    out_copy.wait()

    tile = finish_round(2)
    sums = jnp.sum(tile, axis=-1, keepdims=True)
    loss_ref[...] = DS * sums[0:1] / sums[1:2]
    all_of(2, ar_send).wait()


def per_device(student, teacher, counts, plan):
    n_group = lax.axis_size("group")
    n_member = lax.axis_size("member")
    any_space = pl.BlockSpec(memory_space=pl.ANY)
    hbm = pl.BlockSpec(memory_space=pltpu.HBM)
    vmem = pl.BlockSpec(memory_space=pltpu.VMEM)
    dma = pltpu.SemaphoreType.DMA
    grad, loss = pl.pallas_call(
        functools.partial(kernel, n_group, n_member),
        out_shape=(
            jax.ShapeDtypeStruct((ROWS, DS), F32),
            jax.ShapeDtypeStruct((1, 1), F32),
        ),
        in_specs=[hbm, hbm, hbm, hbm],
        out_specs=(any_space, vmem),
        scratch_shapes=[
            pltpu.VMEM((ROWS, DS), BF16),
            pltpu.VMEM((ROWS, DT), BF16),
            pltpu.VMEM((ROWS,), jnp.int32),
            pltpu.SMEM((1, 1, 5), jnp.int32),
            pltpu.SMEM((6,), F32),
            pltpu.VMEM((6, ROWS, DU), BF16),
            pltpu.VMEM((ROWS, DU), BF16),
            pltpu.VMEM((ROWS, DS), F32),
            pltpu.VMEM((ROWS, 1), F32),
            pltpu.VMEM((ROWS, THIRD), F32),
            pltpu.VMEM((6, 3, 8, THIRD), F32),
            pltpu.VMEM((8, 2 * THIRD), F32),
            pltpu.VMEM((3, 16, 8, THIRD), F32),
            pltpu.VMEM((ROWS, DS), F32),
            dma((3, 3)),
            dma((4, NC)),
            dma((4, NC)),
            dma((3,)),
            dma((3,)),
            dma((5,)),
            dma((5,)),
            dma((3,)),
            dma((3,)),
            dma,
            pltpu.SemaphoreType.REGULAR((6,)),
        ],
        compiler_params=pltpu.CompilerParams(
            collective_id=0, has_side_effects=True, vmem_limit_bytes=62 * 1024 * 1024
        ),
    )(student, teacher, counts, plan)
    return grad, loss.reshape(())


def solution(mesh):
    return jax.shard_map(
        per_device,
        mesh=mesh,
        in_specs=(
            P(("group", "member"), None),
            P(("group", "member"), None),
            P(("group", "member")),
            P("group", "member", None),
        ),
        out_specs=(P(("group", "member"), None), P()),
        check_vma=False,
    )
```

time: 102 us -> 82.4 us (0.81)
  Pallas kernels: 94.4 us -> 76.5 us
  local copies, waits for them, and re-layouts: 4.55 us -> 2.36 us
    pallas_call x1, Pallas kernels: 94.4 us -> 76.5 us  [per_device(): pl.pallas_call(functools.partial(kernel, n_group, n_member), out_shape=(j...]
    unnamed x7 -> x1, local copies, waits for them, and re-layouts: 3.87 us -> 2.36 us
where the time goes in v2:
time: 82.4 us; the launch traced here: 81.2 us
  Pallas kernels  76.5 us (93%)
  between operations  2.39 us (3%)
  local copies, waits for them, and re-layouts  2.36 us (3%)
    pallas_call x1, Pallas kernels, per_device(): pl.pallas_call(functools.partial(kernel, n_group, n_member), out_shape=(j...  76.5 us
    unnamed x1, local copies, waits for them, and re-layouts  2.36 us

profile of v2, /device:TPU:1, one launch (start us, length us, event | category | flops | bytes accessed | tf_op | source)
XLA Modules:
  0.0 81.2 jit_solution(8080316055536462427)
XLA Ops:
  0.6 76.5 %shard_map.59 = (f32[384,768]{1,0:T(8,128)}, f32[1,1]{1,0:T(1,128)}) custom-call(bf16[384,768]{1,0:T(8,128)(2,1)} %s_hbm.1, bf16[384,1024]{1,0:T(8,128)(2,1)} %t_hbm.1, s32[384]{0:T(512)} %c_hbm.1, s32[1,1,5]{2,1,0:T(1,128)} %plan_hbm.1), custom_call_target="tpu_custom_call" | custom-call | tf_op jit(solution)/shard_map/pallas_call | solution.py:325
  77.1 2.4 %copy.8 = f32[384,768]{1,0:T(8,128)} copy(f32[384,768]{1,0:T(8,128)} %get-tuple-element.8) | data formatting | bytes 2359296

commit v3 on v2

--- a/solution.py
+++ b/solution.py
@@ -136,15 +136,14 @@
                 wcol[pl.ds(part * THIRD, THIRD), :] = wide.T
                 wbuf[0, part] = jnp.broadcast_to(row, (8, THIRD))
             pl.semaphore_wait(barrier, len(near))
+            w_copy(0).start()
+            w_copy(4).start()
 
         @pl.loop(third * PER_THIRD, (third + 1) * PER_THIRD)
         def _(k):
             block_copy(0, k).start()
 
         to_core(third).start()
-        if third == 0:
-            w_copy(0).start()
-            w_copy(4).start()
 
     acc[...] = jnp.zeros_like(acc)
     lossacc[...] = jnp.zeros_like(lossacc)
@@ -358,9 +357,9 @@
             pltpu.SemaphoreType.REGULAR((6,)),
         ],
         compiler_params=pltpu.CompilerParams(
-            collective_id=0, has_side_effects=True, vmem_limit_bytes=62 * 1024 * 1024
+            collective_id=0, has_side_effects=True, vmem_limit_bytes=48 * 1024 * 1024
         ),
-    )(student, teacher, counts, plan)
+    )(*(pltpu.with_memory_space_constraint(a, pltpu.HBM) for a in (student, teacher, counts, plan)))
     return grad, loss.reshape(())
 
 

time: 82.4 us -> 73.3 us (0.89)
  Pallas kernels: 76.5 us -> 69 us
  local copies, waits for them, and re-layouts: 2.36 us -> 1.02 us
    pallas_call x1, Pallas kernels: 76.5 us -> 69 us  [per_device(): pl.pallas_call(functools.partial(kernel, n_group, n_member), out_shape=(j...]
    unnamed x1, local copies, waits for them, and re-layouts: 2.36 us -> 1.02 us
where the time goes in v3:
time: 73.3 us; the launch traced here: 72.4 us
  Pallas kernels  69 us (94%)
  between operations  2.33 us (3%)
  local copies, waits for them, and re-layouts  1.02 us (1%)
    pallas_call x1, Pallas kernels, per_device(): pl.pallas_call(functools.partial(kernel, n_group, n_member), out_shape=(j...  69 us

profile of v3, /device:TPU:1, one launch (start us, length us, event | category | flops | bytes accessed | tf_op | source)
XLA Modules:
  0.0 72.4 jit_solution(17024750280257775843)
XLA Ops:
  0.6 69.0 %shard_map.59 = (f32[384,768]{1,0:T(8,128)S(1)}, f32[1,1]{1,0:T(1,128)}) custom-call(bf16[384,768]{1,0:T(8,128)(2,1)} %s_hbm.1, bf16[384,1024]{1,0:T(8,128)(2,1)} %t_hbm.1, s32[384]{0:T(512)} %c_hbm.1, s32[1,1,5]{2,1,0:T(1,128)} %plan_hbm.1), custom_call_target="tpu_custom_call" | custom-call | tf_op jit(solution)/shard_map/pallas_call | solution.py:324
  69.7 1.0 %copy.8 = f32[384,768]{1,0:T(8,128)} copy(f32[384,768]{1,0:T(8,128)S(1)} %get-tuple-element.8) | data formatting | bytes 2359296

commit v4 on v3

--- a/solution.py
+++ b/solution.py
@@ -16,13 +16,19 @@
 DU = DS + DT
 THIRD = 128
 CHUNK = 16
-NC = ROWS // CHUNK
-PER_THIRD = NC // 3
-LAG_Q, LAG_R, LAG_F = 3, 6, 8
+SHORT = 8
+HEAD = 0
+EXTRA = HEAD - HEAD * SHORT // CHUNK
+NC = ROWS // CHUNK + EXTRA
+PER_THIRD = THIRD // CHUNK
+FIRST = NC - 2 * PER_THIRD
+LAG_Q, LAG_R, LAG_F = 4, 8, 10
 STEPS = NC + LAG_F
 EARLY = 3
+LOSS_STEP = LAG_Q + NC - 1
 TOKENS = 8
 NORM = 32
+PARTS = ((0, NORM), (NORM, THIRD), (THIRD, 2 * THIRD), (2 * THIRD, ROWS))
 F32 = jnp.float32
 BF16 = jnp.bfloat16
 
@@ -31,8 +37,8 @@
     n_group, n_member,
     s_hbm, t_hbm, c_hbm, plan_hbm,
     grad_hbm, loss_ref,
-    s_in, t_in, c_in, plan_in, switches, slots, lhs, acc, scale, wcol, wbuf, lossacc, tiles, out_buf,
-    in_sem, send, recv, xsend, xrecv, wsend, wrecv, ar_send, ar_recv, out_sem, tokens,
+    s_in, t_in, c_in, plan_in, switches, slots, lhs, acc, coef, scale, wcol, mixcol, wbuf, lossacc, tiles, out_buf,
+    in_sem, send, recv, xsend, xrecv, nsend, nrecv, wsend, wrecv, ar_send, ar_recv, out_sem, tokens,
 ):
     g = lax.axis_index("group")
     m = lax.axis_index("member")
@@ -57,10 +63,10 @@
         pltpu.make_async_copy(plan_hbm, plan_in, in_sem.at[2, 1]),
     ]
     copies = []
-    for third in range(3):
-        rows = pl.ds(third * THIRD, THIRD)
+    for part, (low, high) in enumerate(PARTS):
+        rows = pl.ds(low, high - low)
         for which, (src, dst) in enumerate(((s_hbm, s_in), (t_hbm, t_in))):
-            copies.append(pltpu.make_async_copy(src.at[rows], dst.at[rows], in_sem.at[which, third]))
+            copies.append(pltpu.make_async_copy(src.at[rows], dst.at[rows], in_sem.at[which, part]))
     for copy in copies[:2] + small + copies[2:]:
         copy.start()
 
@@ -72,7 +78,8 @@
         (device(g, m_up), 3), (device(g, m_down), 2),
         (device(g_up, m), 5), (device(g_down, m), 4),
     ]
-    near = [peer for peer, _ in sides] + [device(g, m_core)]
+    m_diagonal = (1 - core) * (m_down + 1) + core * (m_up - 1)
+    near = [peer for peer, _ in sides] + [device(g, m_core), device(g, m_diagonal)]
     for peer in near:
         pl.semaphore_signal(barrier, inc=1, device_id=peer, device_id_type=MESH)
 
@@ -94,9 +101,12 @@
         (0, 2, xor_peer), (2, 3, x_other), (3, 4, device(g, m_z)), (3 + role, 5, device(g, m_core)),
     ]
 
-    def block_copy(flow, k):
+    def block_copy(flow, k, short):
         src, dst, to = flows[flow]
-        rows = pl.ds(pl.multiple_of(k * CHUNK, CHUNK), CHUNK)
+        if short:
+            rows = pl.ds(pl.multiple_of(k * SHORT, SHORT), SHORT)
+        else:
+            rows = pl.ds(pl.multiple_of(k * CHUNK - HEAD * (CHUNK - SHORT), CHUNK), CHUNK)
         return pltpu.make_async_remote_copy(
             src_ref=slots.at[src, rows], dst_ref=slots.at[dst, rows],
             send_sem=send.at[flow, k], recv_sem=recv.at[flow, k],
@@ -104,7 +114,7 @@
         )
 
     def w_copy(flow):
-        src, dst, to = (flows + [(0, 1, device(g, m_core))])[flow]
+        src, dst, to = (flows + [(0, 1, device(g, m_core)), (0, 6, n_peer)])[flow]
         return pltpu.make_async_remote_copy(
             src_ref=wbuf.at[src], dst_ref=wbuf.at[dst],
             send_sem=wsend.at[flow], recv_sem=wrecv.at[flow],
@@ -119,39 +129,70 @@
             device_id=device(g, m_core), device_id_type=MESH,
         )
 
-    for third in range(3):
-        copies[2 * third].wait()
-        copies[2 * third + 1].wait()
-
-        @pl.loop(third * (THIRD // NORM), (third + 1) * (THIRD // NORM))
-        def _(k):
-            normalise(k)
-
-        if third == 0:
+    n_peer = device(g, x_hi * m_up + (1 - x_hi) * m_diagonal)
+    n_sends = x_hi + (1 - x_hi) * (1 - core)
+    n_takes = x_hi + (1 - x_hi) * core
+    mix = 6 * n_takes + (1 - n_takes)
+
+    def to_mix(third):
+        rows = pl.ds(third * THIRD, THIRD)
+        return pltpu.make_async_remote_copy(
+            src_ref=slots.at[0, rows], dst_ref=slots.at[6, rows],
+            send_sem=nsend.at[third], recv_sem=nrecv.at[third],
+            device_id=n_peer, device_id_type=MESH,
+        )
+
+    columns = [2 - 2 * core, 4 + 0 * core, 3 - 2 * x_hi, 1 + 2 * x_hi, 2 * core]
+
+    def switch_of(slot):
+        return plan_in[0, 0, columns[slot - 1]].astype(F32)
+
+    per_norm = NORM // CHUNK
+    for part, (low, high) in enumerate(PARTS):
+        copies[2 * part].wait()
+        copies[2 * part + 1].wait()
+        if part == 0:
+            normalise(0)
             for copy in small:
                 copy.wait()
-            for part in range(3):
-                row = c_in[pl.ds(part * THIRD, THIRD)].astype(F32).reshape(1, THIRD)
-                wide = jnp.broadcast_to(row, (THIRD, THIRD))
-                wcol[pl.ds(part * THIRD, THIRD), :] = wide.T
-                wbuf[0, part] = jnp.broadcast_to(row, (8, THIRD))
+            for third in range(3):
+                row = c_in[pl.ds(third * THIRD, THIRD)].astype(F32).reshape(1, THIRD)
+                wbuf[0, third] = jnp.broadcast_to(row, (8, THIRD))
+            for i in range(2):
+                wbuf[0, 3 + i] = jnp.full((8, THIRD), switch_of(4 + i), F32)
             pl.semaphore_wait(barrier, len(near))
             w_copy(0).start()
             w_copy(4).start()
 
-        @pl.loop(third * PER_THIRD, (third + 1) * PER_THIRD)
-        def _(k):
-            block_copy(0, k).start()
-
-        to_core(third).start()
-
+            @pl.when(n_sends == 1)
+            def _():
+                w_copy(5).start()
+
+            for k in range(HEAD or per_norm):
+                block_copy(0, k, HEAD > 0).start()
+        else:
+            @pl.loop(low // NORM, high // NORM)
+            def _(n):
+                normalise(n)
+                for i in range(per_norm):
+                    block_copy(0, n * per_norm + i + EXTRA, False).start()
+
+        if part >= 1:
+            to_core(part - 1).start()
+
+            @pl.when(n_sends == 1)
+            def _():
+                to_mix(part - 1).start()
+
+    for third in range(3):
+        wide = jnp.broadcast_to(wbuf[0, third, 0:1], (THIRD, THIRD))
+        wcol[pl.ds(third * THIRD, THIRD), :] = wide.T
     acc[...] = jnp.zeros_like(acc)
     lossacc[...] = jnp.zeros_like(lossacc)
 
-    columns = [2 - 2 * core, 4 + 0 * core, 3 - 2 * x_hi, 1 + 2 * x_hi, 2 * core]
     switches[0] = jnp.float32(1.0)
     for slot in range(5):
-        switches[slot + 1] = plan_in[0, 0, columns[slot]].astype(F32)
+        switches[slot + 1] = switch_of(slot + 1)
     w_copy(4).wait_recv()
 
     def piece(pair, third):
@@ -165,9 +206,31 @@
         )[0:1]
         w_i = wcol[...]
         weighted = jnp.concatenate([w_i, w_i], axis=1) * w_j * diff
-        loss = weighted * diff
-        lossacc[...] += jnp.sum(loss.reshape(ROWS // 8, 8, 2 * THIRD), axis=0)
-        acc[...] += jnp.dot(weighted.astype(BF16), both[:, 0:DS], preferred_element_type=F32)
+        if pair < 2:
+            loss = weighted * diff
+            lossacc[...] += jnp.sum(loss.reshape(ROWS // 8, 8, 2 * THIRD), axis=0)
+        coef[...] = weighted.astype(BF16)
+
+    def gradient(pair, third):
+        rows = pl.ds(pl.multiple_of(third * THIRD, THIRD), THIRD)
+        both = jnp.concatenate(
+            [slots[2 * pair, rows, 0:DS], slots[2 * pair + 1, rows, 0:DS]], axis=0
+        )
+        acc[...] += jnp.dot(coef[...], both, preferred_element_type=F32)
+
+    def mixed(i0, i1, j0, j1):
+        left, right = pl.ds(i0 * THIRD, (i1 - i0) * THIRD), pl.ds(j0 * THIRD, (j1 - j0) * THIRD)
+        nt = (((1,), (1,)), ((), ()))
+        diff = lax.dot_general(
+            slots[mix, left, 0:DS], slots[3, right, 0:DS], nt, preferred_element_type=F32
+        ) - lax.dot_general(
+            slots[mix, left, DS:DU], slots[3, right, DS:DU], nt, preferred_element_type=F32
+        )
+        w_j = jnp.concatenate([wbuf[3, j] for j in range(j0, j1)], axis=1)[0:1]
+        w_i = jnp.concatenate([mixcol[left, :]] * (j1 - j0), axis=1)
+        loss = w_i * w_j * diff * diff
+        width = (j1 - j0) * THIRD
+        lossacc[:, 0:width] += jnp.sum(loss.reshape((i1 - i0) * THIRD // 8, 8, width), axis=0)
 
     def signal_sides():
         for peer, place in sides:
@@ -177,61 +240,17 @@
         for place in range(6):
             pl.semaphore_wait(tokens.at[place], 1)
 
-    @pl.loop(0, STEPS)
-    def _(k):
-        @pl.when(k < NC)
-        def _():
-            block_copy(0, k).wait_recv()
-            block_copy(1, k).start()
-
-        for flow, lag in ((1, LAG_Q), (2, LAG_R)):
-            @pl.when((k >= lag) & (k < NC + lag))
-            def _():
-                block_copy(flow, k - lag).wait_recv()
-                block_copy(flow + 1, k - lag).start()
-
-        @pl.when(k >= LAG_F)
-        def _():
-            block_copy(3, k - LAG_F).wait_recv()
-
-        for flow, lag in enumerate((0, LAG_Q, LAG_R, LAG_F)):
-            @pl.when(k == lag)
-            def _():
-                w_copy(flow).wait_recv()
-                if flow < 3:
-                    w_copy(flow + 1).start()
-
-        @pl.when((k >= 2) & (k < 2 + TOKENS))
-        def _():
-            signal_sides()
-
-        @pl.when((k >= 4) & (k < 4 + TOKENS))
-        def _():
-            wait_sides()
-
-        @pl.when((k < 2 * EARLY) & (lax.rem(k, 2) == 0))
-        def _():
-            to_core(k // 2).wait_recv()
-            piece(0, k // 2)
-
-        ready = (LAG_Q + PER_THIRD - 1, LAG_F + PER_THIRD - 1)
-        for pair in range(2):
-            late = k - ready[pair]
-
-            @pl.when((late >= 0) & (lax.rem(late + 3 * NC, PER_THIRD) == 0) & (late < NC))
-            def _():
-                piece(1 + pair, late // PER_THIRD)
-
-    total_w = jnp.zeros((8, THIRD), F32)
-    own_w = jnp.zeros((8, THIRD), F32)
-    for third in range(3):
-        own_w = own_w + wbuf[0, third]
-        for slot in range(6):
-            total_w = total_w + wbuf[slot, third] * switches[slot]
-    weight_lanes = total_w * jnp.sum(own_w, axis=-1, keepdims=True)
-    loss_lanes = jnp.sum(lossacc[:, 0:THIRD] + lossacc[:, THIRD:], axis=0, keepdims=True)
-    row_id = lax.broadcasted_iota(jnp.int32, (8, THIRD), 0)
-    tile = jnp.where(row_id == 0, jnp.broadcast_to(loss_lanes, (8, THIRD)), weight_lanes)
+    def partial_sums():
+        total_w = jnp.zeros((8, THIRD), F32)
+        own_w = jnp.zeros((8, THIRD), F32)
+        for third in range(3):
+            own_w = own_w + wbuf[0, third]
+            for slot in range(6):
+                total_w = total_w + wbuf[slot, third] * switches[slot]
+        weight_lanes = total_w * jnp.sum(own_w, axis=-1, keepdims=True)
+        loss_lanes = jnp.sum(lossacc[:, 0:THIRD] + lossacc[:, THIRD:], axis=0, keepdims=True)
+        row_id = lax.broadcasted_iota(jnp.int32, (8, THIRD), 0)
+        return jnp.where(row_id == 0, jnp.broadcast_to(loss_lanes, (8, THIRD)), weight_lanes)
 
     y = g // 2
     z = m // 4
@@ -277,9 +296,99 @@
             total = total + tiles[r, d]
         return total
 
-    send_round(0, tile)
-    tile = finish_round(0)
-    send_round(1, tile)
+    def pass_on(k, short):
+        if short:
+            active = lambda i: (i >= 0) & (i < HEAD)
+        else:
+            active = lambda i: (i >= HEAD) & (i < NC)
+        for flow, lag in enumerate((0, LAG_Q, LAG_R, LAG_F)):
+            @pl.when(active(k - lag))
+            def _():
+                block_copy(flow, k - lag, short).wait_recv()
+                if flow < 3:
+                    block_copy(flow + 1, k - lag, short).start()
+
+    def products(k):
+        @pl.when((k >= 3) & (k < 3 + TOKENS))
+        def _():
+            wait_sides()
+
+        @pl.when((k >= 2) & (k < 2 + TOKENS))
+        def _():
+            signal_sides()
+
+        @pl.when((k < 2 * EARLY) & (lax.rem(k, 2) == 0))
+        def _():
+            to_core(k // 2).wait_recv()
+            piece(0, k // 2)
+            gradient(0, k // 2)
+
+        for pair, lag in ((1, LAG_Q), (2, LAG_F)):
+            late = k - lag - (FIRST - 1)
+
+            @pl.when((late >= 0) & (lax.rem(late + 3 * PER_THIRD, PER_THIRD) == 0) & (k < STEPS - 1))
+            def _():
+                piece(pair, late // PER_THIRD)
+                if pair == 2:
+                    gradient(pair, late // PER_THIRD)
+                else:
+                    @pl.when(k < LOSS_STEP)
+                    def _():
+                        gradient(pair, late // PER_THIRD)
+
+        @pl.when(k == LOSS_STEP - PER_THIRD)
+        def _():
+            @pl.when(n_takes == 1)
+            def _():
+                w_copy(5).wait_recv()
+                to_mix(0).wait_recv()
+                to_mix(1).wait_recv()
+
+            factor = 2.0 * wbuf[mix, 4 - x_hi][0:1]
+            for third in range(3):
+                wide = jnp.broadcast_to(wbuf[mix, third][0:1] * factor, (THIRD, THIRD))
+                mixcol[pl.ds(third * THIRD, THIRD), :] = wide.T
+            mixed(0, 2, 0, 2)
+
+        @pl.when(k == LOSS_STEP - 1)
+        def _():
+            @pl.when(n_takes == 1)
+            def _():
+                to_mix(2).wait_recv()
+
+            mixed(2, 3, 0, 2)
+
+        @pl.when(k == LOSS_STEP)
+        def _():
+            mixed(0, 3, 2, 3)
+            send_round(0, partial_sums())
+            gradient(1, 2)
+
+        @pl.when(k == LOSS_STEP + 1)
+        def _():
+            send_round(1, finish_round(0))
+
+    @pl.loop(0, STEPS)
+    def _(k):
+        if HEAD:
+            @pl.when(k < HEAD + LAG_F)
+            def _():
+                pass_on(k, True)
+
+        pass_on(k, False)
+
+        for flow, lag in enumerate((0, LAG_Q, LAG_R, LAG_F)):
+            @pl.when(k == lag)
+            def _():
+                w_copy(flow).wait_recv()
+                if flow < 3:
+                    w_copy(flow + 1).start()
+
+        products(k)
+
+    send_round(2, finish_round(1))
+    piece(2, 2)
+    gradient(2, 2)
 
     @pl.loop(0, ROWS // NORM)
     def _(k):
@@ -292,18 +401,23 @@
     out_copy = pltpu.make_async_copy(out_buf, grad_hbm, out_sem)
     out_copy.start()
 
-    tile = finish_round(1)
-    send_round(2, tile)
-
-    @pl.loop(0, NC)
-    def _(k):
-        for flow in range(4):
-            block_copy(flow, k).wait_send()
+    for low, high in ((0, HEAD), (HEAD, NC)) if HEAD else ((0, NC),):
+        @pl.loop(low, high)
+        def _(k):
+            for flow in range(4):
+                block_copy(flow, k, high == HEAD).wait_send()
 
     for third in range(3):
         to_core(third).wait_send()
     for flow in range(5):
         w_copy(flow).wait_send()
+
+    @pl.when(n_sends == 1)
+    def _():
+        w_copy(5).wait_send()
+        for third in range(3):
+            to_mix(third).wait_send()
+
     for r in range(2):
         all_of(r, ar_send).wait()
     out_copy.wait()
@@ -335,22 +449,26 @@
             pltpu.VMEM((ROWS,), jnp.int32),
             pltpu.SMEM((1, 1, 5), jnp.int32),
             pltpu.SMEM((6,), F32),
-            pltpu.VMEM((6, ROWS, DU), BF16),
+            pltpu.VMEM((7, ROWS, DU), BF16),
             pltpu.VMEM((ROWS, DU), BF16),
             pltpu.VMEM((ROWS, DS), F32),
+            pltpu.VMEM((ROWS, 2 * THIRD), BF16),
             pltpu.VMEM((ROWS, 1), F32),
             pltpu.VMEM((ROWS, THIRD), F32),
-            pltpu.VMEM((6, 3, 8, THIRD), F32),
+            pltpu.VMEM((ROWS, THIRD), F32),
+            pltpu.VMEM((7, 5, 8, THIRD), F32),
             pltpu.VMEM((8, 2 * THIRD), F32),
             pltpu.VMEM((3, 16, 8, THIRD), F32),
             pltpu.VMEM((ROWS, DS), F32),
-            dma((3, 3)),
+            dma((3, 4)),
             dma((4, NC)),
             dma((4, NC)),
             dma((3,)),
             dma((3,)),
-            dma((5,)),
-            dma((5,)),
+            dma((3,)),
+            dma((3,)),
+            dma((6,)),
+            dma((6,)),
             dma((3,)),
             dma((3,)),
             dma,

time: 73.3 us -> 71.7 us (0.978)
  Pallas kernels: 69 us -> 68.2 us
    pallas_call x1, Pallas kernels: 69 us -> 68.2 us  [per_device(): pl.pallas_call(functools.partial(kernel, n_group, n_member), out_shape=(j...]
where the time goes in v4:
time: 71.7 us; the launch traced here: 71.5 us
  Pallas kernels  68.2 us (95%)
  between operations  2.33 us (3%)
  local copies, waits for them, and re-layouts  1.02 us (1%)
    pallas_call x1, Pallas kernels, per_device(): pl.pallas_call(functools.partial(kernel, n_group, n_member), out_shape=(j...  68.2 us

profile of v4, /device:TPU:1, one launch (start us, length us, event | category | flops | bytes accessed | tf_op | source)
XLA Modules:
  0.0 71.5 jit_solution(8626241617829882875)
XLA Ops:
  0.6 68.2 %shard_map.59 = (f32[384,768]{1,0:T(8,128)S(1)}, f32[1,1]{1,0:T(1,128)}) custom-call(bf16[384,768]{1,0:T(8,128)(2,1)} %s_hbm.1, bf16[384,1024]{1,0:T(8,128)(2,1)} %t_hbm.1, s32[384]{0:T(512)} %c_hbm.1, s32[1,1,5]{2,1,0:T(1,128)} %plan_hbm.1), custom_call_target="tpu_custom_call" | custom-call | tf_op jit(solution)/shard_map/pallas_call | solution.py:438
  68.8 1.0 %copy.8 = f32[384,768]{1,0:T(8,128)} copy(f32[384,768]{1,0:T(8,128)S(1)} %get-tuple-element.8) | data formatting | bytes 2359296

commit v5 on v4

--- a/solution.py
+++ b/solution.py
@@ -206,9 +206,9 @@
         )[0:1]
         w_i = wcol[...]
         weighted = jnp.concatenate([w_i, w_i], axis=1) * w_j * diff
-        if pair < 2:
-            loss = weighted * diff
-            lossacc[...] += jnp.sum(loss.reshape(ROWS // 8, 8, 2 * THIRD), axis=0)
+        counted = jnp.where(pair == 2, 0.0, 1.0)
+        loss = weighted * diff
+        lossacc[...] += counted * jnp.sum(loss.reshape(ROWS // 8, 8, 2 * THIRD), axis=0)
         coef[...] = weighted.astype(BF16)
 
     def gradient(pair, third):
@@ -218,19 +218,30 @@
         )
         acc[...] += jnp.dot(coef[...], both, preferred_element_type=F32)
 
-    def mixed(i0, i1, j0, j1):
-        left, right = pl.ds(i0 * THIRD, (i1 - i0) * THIRD), pl.ds(j0 * THIRD, (j1 - j0) * THIRD)
+    def mixed(third):
+        right = pl.ds(pl.multiple_of(third * THIRD, THIRD), THIRD)
         nt = (((1,), (1,)), ((), ()))
         diff = lax.dot_general(
-            slots[mix, left, 0:DS], slots[3, right, 0:DS], nt, preferred_element_type=F32
+            slots[mix, :, 0:DS], slots[3, right, 0:DS], nt, preferred_element_type=F32
         ) - lax.dot_general(
-            slots[mix, left, DS:DU], slots[3, right, DS:DU], nt, preferred_element_type=F32
-        )
-        w_j = jnp.concatenate([wbuf[3, j] for j in range(j0, j1)], axis=1)[0:1]
-        w_i = jnp.concatenate([mixcol[left, :]] * (j1 - j0), axis=1)
-        loss = w_i * w_j * diff * diff
-        width = (j1 - j0) * THIRD
-        lossacc[:, 0:width] += jnp.sum(loss.reshape((i1 - i0) * THIRD // 8, 8, width), axis=0)
+            slots[mix, :, DS:DU], slots[3, right, DS:DU], nt, preferred_element_type=F32
+        )
+        loss = mixcol[...] * wbuf[3, third][0:1] * diff * diff
+        lossacc[:, 0:THIRD] += jnp.sum(loss.reshape(ROWS // 8, 8, THIRD), axis=0)
+
+    def planned(k):
+        first = (k >= 0) & (k < 2 * EARLY) & (lax.rem(k + 2, 2) == 0)
+        active = jnp.where(first, 1, 0)
+        pair = 0
+        third = active * (k // 2)
+        for p, lag in ((1, LAG_Q), (2, LAG_F)):
+            late = jnp.maximum(k - (lag + FIRST - 1), 0)
+            due = (k >= lag + FIRST - 1) & (lax.rem(late, PER_THIRD) == 0) & (late < 3 * PER_THIRD)
+            due = jnp.where(due, 1, 0)
+            active = active + due
+            pair = pair + p * due
+            third = third + due * (late // PER_THIRD)
+        return active == 1, pair, third
 
     def signal_sides():
         for peer, place in sides:
@@ -309,66 +320,63 @@
                     block_copy(flow + 1, k - lag, short).start()
 
     def products(k):
-        @pl.when((k >= 3) & (k < 3 + TOKENS))
+        @pl.when((k >= 4) & (k < 4 + 2 * TOKENS) & (lax.rem(k, 2) == 0))
         def _():
             wait_sides()
 
-        @pl.when((k >= 2) & (k < 2 + TOKENS))
+        @pl.when((k >= 2) & (k < 2 + 2 * TOKENS) & (lax.rem(k, 2) == 0))
         def _():
             signal_sides()
-
-        @pl.when((k < 2 * EARLY) & (lax.rem(k, 2) == 0))
-        def _():
-            to_core(k // 2).wait_recv()
-            piece(0, k // 2)
-            gradient(0, k // 2)
-
-        for pair, lag in ((1, LAG_Q), (2, LAG_F)):
-            late = k - lag - (FIRST - 1)
-
-            @pl.when((late >= 0) & (lax.rem(late + 3 * PER_THIRD, PER_THIRD) == 0) & (k < STEPS - 1))
-            def _():
-                piece(pair, late // PER_THIRD)
-                if pair == 2:
-                    gradient(pair, late // PER_THIRD)
-                else:
-                    @pl.when(k < LOSS_STEP)
-                    def _():
-                        gradient(pair, late // PER_THIRD)
 
         @pl.when(k == LOSS_STEP - PER_THIRD)
         def _():
             @pl.when(n_takes == 1)
             def _():
                 w_copy(5).wait_recv()
-                to_mix(0).wait_recv()
-                to_mix(1).wait_recv()
 
             factor = 2.0 * wbuf[mix, 4 - x_hi][0:1]
             for third in range(3):
                 wide = jnp.broadcast_to(wbuf[mix, third][0:1] * factor, (THIRD, THIRD))
                 mixcol[pl.ds(third * THIRD, THIRD), :] = wide.T
-            mixed(0, 2, 0, 2)
-
-        @pl.when(k == LOSS_STEP - 1)
-        def _():
-            @pl.when(n_takes == 1)
-            def _():
-                to_mix(2).wait_recv()
-
-            mixed(2, 3, 0, 2)
+
+        @pl.when((k == LOSS_STEP - 3) & (n_takes == 1))
+        def _():
+            for third in range(3):
+                to_mix(third).wait_recv()
+
+        @pl.when(k == LOSS_STEP + 1)
+        def _():
+            send_round(1, finish_round(0))
+
+        @pl.when(k == NC + LAG_R)
+        def _():
+            send_round(2, finish_round(1))
+
+        @pl.when((k < 2 * EARLY) & (lax.rem(k, 2) == 0))
+        def _():
+            to_core(k // 2).wait_recv()
+
+        before, pair_before, third_before = planned(k - 1)
+
+        @pl.when(before)
+        def _():
+            gradient(pair_before, third_before)
+
+        now, pair_now, third_now = planned(k)
+
+        @pl.when(now)
+        def _():
+            piece(pair_now, third_now)
+
+        @pl.when((k == LOSS_STEP - 3) | (k == LOSS_STEP - 1) | (k == LOSS_STEP))
+        def _():
+            mixed(jnp.maximum(k - (LOSS_STEP - 2), 0))
 
         @pl.when(k == LOSS_STEP)
         def _():
-            mixed(0, 3, 2, 3)
             send_round(0, partial_sums())
-            gradient(1, 2)
-
-        @pl.when(k == LOSS_STEP + 1)
-        def _():
-            send_round(1, finish_round(0))
-
-    @pl.loop(0, STEPS)
+
+    @pl.loop(0, STEPS + 1)
     def _(k):
         if HEAD:
             @pl.when(k < HEAD + LAG_F)
@@ -385,10 +393,6 @@
                     w_copy(flow + 1).start()
 
         products(k)
-
-    send_round(2, finish_round(1))
-    piece(2, 2)
-    gradient(2, 2)
 
     @pl.loop(0, ROWS // NORM)
     def _(k):

time: 71.7 us -> 70.1 us (0.978)
  Pallas kernels: 68.2 us -> 66.6 us
    pallas_call x1, Pallas kernels: 68.2 us -> 66.6 us  [per_device(): pl.pallas_call(functools.partial(kernel, n_group, n_member), out_shape=(j...]
where the time goes in v5:
time: 70.1 us; the launch traced here: 69.9 us
  Pallas kernels  66.6 us (95%)
  between operations  2.33 us (3%)
  local copies, waits for them, and re-layouts  1.02 us (1%)
    pallas_call x1, Pallas kernels, per_device(): pl.pallas_call(functools.partial(kernel, n_group, n_member), out_shape=(j...  66.6 us

profile of v5, /device:TPU:1, one launch (start us, length us, event | category | flops | bytes accessed | tf_op | source)
XLA Modules:
  0.0 69.9 jit_solution(1688386562563049508)
XLA Ops:
  0.6 66.6 %shard_map.59 = (f32[384,768]{1,0:T(8,128)S(1)}, f32[1,1]{1,0:T(1,128)}) custom-call(bf16[384,768]{1,0:T(8,128)(2,1)} %s_hbm.1, bf16[384,1024]{1,0:T(8,128)(2,1)} %t_hbm.1, s32[384]{0:T(512)} %c_hbm.1, s32[1,1,5]{2,1,0:T(1,128)} %plan_hbm.1), custom_call_target="tpu_custom_call" | custom-call | tf_op jit(solution)/shard_map/pallas_call | solution.py:442
  67.2 1.0 %copy.8 = f32[384,768]{1,0:T(8,128)} copy(f32[384,768]{1,0:T(8,128)S(1)} %get-tuple-element.8) | data formatting | bytes 2359296

commit v6 on v5

--- a/solution.py
+++ b/solution.py
@@ -22,10 +22,11 @@
 NC = ROWS // CHUNK + EXTRA
 PER_THIRD = THIRD // CHUNK
 FIRST = NC - 2 * PER_THIRD
-LAG_Q, LAG_R, LAG_F = 4, 8, 10
+LAG_Q, LAG_R, LAG_F = 3, 7, 9
 STEPS = NC + LAG_F
 EARLY = 3
 LOSS_STEP = LAG_Q + NC - 1
+Z_STEP = LOSS_STEP + 3
 TOKENS = 8
 NORM = 32
 PARTS = ((0, NORM), (NORM, THIRD), (THIRD, 2 * THIRD), (2 * THIRD, ROWS))
@@ -344,14 +345,6 @@
             for third in range(3):
                 to_mix(third).wait_recv()
 
-        @pl.when(k == LOSS_STEP + 1)
-        def _():
-            send_round(1, finish_round(0))
-
-        @pl.when(k == NC + LAG_R)
-        def _():
-            send_round(2, finish_round(1))
-
         @pl.when((k < 2 * EARLY) & (lax.rem(k, 2) == 0))
         def _():
             to_core(k // 2).wait_recv()
@@ -378,6 +371,14 @@
 
     @pl.loop(0, STEPS + 1)
     def _(k):
+        @pl.when(k == LOSS_STEP + 1)
+        def _():
+            send_round(1, finish_round(0))
+
+        @pl.when(k == Z_STEP)
+        def _():
+            send_round(2, finish_round(1))
+
         if HEAD:
             @pl.when(k < HEAD + LAG_F)
             def _():

time: 70.1 us -> 68.8 us (0.981)
  Pallas kernels: 66.6 us -> 65.3 us
    pallas_call x1, Pallas kernels: 66.6 us -> 65.3 us  [per_device(): pl.pallas_call(functools.partial(kernel, n_group, n_member), out_shape=(j...]
where the time goes in v6:
time: 68.8 us; the launch traced here: 68.6 us
  Pallas kernels  65.3 us (95%)
  between operations  2.33 us (3%)
  local copies, waits for them, and re-layouts  1.02 us (1%)
    pallas_call x1, Pallas kernels, per_device(): pl.pallas_call(functools.partial(kernel, n_group, n_member), out_shape=(j...  65.3 us

profile of v6, /device:TPU:1, one launch (start us, length us, event | category | flops | bytes accessed | tf_op | source)
XLA Modules:
  0.0 68.6 jit_solution(12153611948298072413)
XLA Ops:
  0.6 65.3 %shard_map.59 = (f32[384,768]{1,0:T(8,128)S(1)}, f32[1,1]{1,0:T(1,128)}) custom-call(bf16[384,768]{1,0:T(8,128)(2,1)} %s_hbm.1, bf16[384,1024]{1,0:T(8,128)(2,1)} %t_hbm.1, s32[384]{0:T(512)} %c_hbm.1, s32[1,1,5]{2,1,0:T(1,128)} %plan_hbm.1), custom_call_target="tpu_custom_call" | custom-call | tf_op jit(solution)/shard_map/pallas_call | solution.py:443
  65.9 1.0 %copy.8 = f32[384,768]{1,0:T(8,128)} copy(f32[384,768]{1,0:T(8,128)S(1)} %get-tuple-element.8) | data formatting | bytes 2359296

commit v7 on v6

--- a/solution.py
+++ b/solution.py
@@ -26,7 +26,7 @@
 STEPS = NC + LAG_F
 EARLY = 3
 LOSS_STEP = LAG_Q + NC - 1
-Z_STEP = LOSS_STEP + 3
+Z_STEP = LOSS_STEP + 2
 TOKENS = 8
 NORM = 32
 PARTS = ((0, NORM), (NORM, THIRD), (THIRD, 2 * THIRD), (2 * THIRD, ROWS))
@@ -68,7 +68,7 @@
         rows = pl.ds(low, high - low)
         for which, (src, dst) in enumerate(((s_hbm, s_in), (t_hbm, t_in))):
             copies.append(pltpu.make_async_copy(src.at[rows], dst.at[rows], in_sem.at[which, part]))
-    for copy in copies[:2] + small + copies[2:]:
+    for copy in copies[:2]:
         copy.start()
 
     barrier = pltpu.get_barrier_semaphore()
@@ -83,6 +83,8 @@
     near = [peer for peer, _ in sides] + [device(g, m_core), device(g, m_diagonal)]
     for peer in near:
         pl.semaphore_signal(barrier, inc=1, device_id=peer, device_id_type=MESH)
+    for copy in small + copies[2:]:
+        copy.start()
 
     def normalise(k):
         rows = pl.ds(pl.multiple_of(k * NORM, NORM), NORM)

time: 68.8 us -> 68.7 us (level)
  no operation moved by 1% of the time
where the time goes in v7:
time: 68.7 us; the launch traced here: 68.6 us
  Pallas kernels  65.2 us (95%)
  between operations  2.33 us (3%)
  local copies, waits for them, and re-layouts  1.02 us (1%)
    pallas_call x1, Pallas kernels, per_device(): pl.pallas_call(functools.partial(kernel, n_group, n_member), out_shape=(j...  65.2 us

profile of v7, /device:TPU:1, one launch (start us, length us, event | category | flops | bytes accessed | tf_op | source)
XLA Modules:
  0.0 68.6 jit_solution(3727726566602962731)
XLA Ops:
  0.6 65.2 %shard_map.59 = (f32[384,768]{1,0:T(8,128)S(1)}, f32[1,1]{1,0:T(1,128)}) custom-call(bf16[384,768]{1,0:T(8,128)(2,1)} %s_hbm.1, bf16[384,1024]{1,0:T(8,128)(2,1)} %t_hbm.1, s32[384]{0:T(512)} %c_hbm.1, s32[1,1,5]{2,1,0:T(1,128)} %plan_hbm.1), custom_call_target="tpu_custom_call" | custom-call | tf_op jit(solution)/shard_map/pallas_call | solution.py:445
  65.8 1.0 %copy.8 = f32[384,768]{1,0:T(8,128)} copy(f32[384,768]{1,0:T(8,128)S(1)} %get-tuple-element.8) | data formatting | bytes 2359296

commit v8 on v6

--- a/solution.py
+++ b/solution.py
@@ -26,7 +26,7 @@
 STEPS = NC + LAG_F
 EARLY = 3
 LOSS_STEP = LAG_Q + NC - 1
-Z_STEP = LOSS_STEP + 3
+Z_STEP = LOSS_STEP + 2
 TOKENS = 8
 NORM = 32
 PARTS = ((0, NORM), (NORM, THIRD), (THIRD, 2 * THIRD), (2 * THIRD, ROWS))

time: 68.8 us -> 68.8 us (level)
  no operation moved by 1% of the time
where the time goes in v8:
time: 68.8 us; the launch traced here: 68.6 us
  Pallas kernels  65.3 us (95%)
  between operations  2.33 us (3%)
  local copies, waits for them, and re-layouts  1.02 us (1%)
    pallas_call x1, Pallas kernels, per_device(): pl.pallas_call(functools.partial(kernel, n_group, n_member), out_shape=(j...  65.3 us

profile of v8, /device:TPU:1, one launch (start us, length us, event | category | flops | bytes accessed | tf_op | source)
XLA Modules:
  0.0 68.6 jit_solution(9953605013148736694)
XLA Ops:
  0.6 65.3 %shard_map.59 = (f32[384,768]{1,0:T(8,128)S(1)}, f32[1,1]{1,0:T(1,128)}) custom-call(bf16[384,768]{1,0:T(8,128)(2,1)} %s_hbm.1, bf16[384,1024]{1,0:T(8,128)(2,1)} %t_hbm.1, s32[384]{0:T(512)} %c_hbm.1, s32[1,1,5]{2,1,0:T(1,128)} %plan_hbm.1), custom_call_target="tpu_custom_call" | custom-call | tf_op jit(solution)/shard_map/pallas_call | solution.py:443
  65.9 1.0 %copy.8 = f32[384,768]{1,0:T(8,128)} copy(f32[384,768]{1,0:T(8,128)S(1)} %get-tuple-element.8) | data formatting | bytes 2359296
